TPU v7x, 256 devices: a whole 4x4x8 slice. The times are simulated.
256 devices in a mesh: dp: 16 (over x, y), tensor: 16 (over z, core).
Axes of the slice: x: 4, y: 4, z: 8, core: 2. Of those that a mesh axis runs over, the one named last changes fastest.
Arguments:
- tokens: bfloat16 [32768, 1280], P(('dp', 'tensor'))
- cotangent: bfloat16 [32768, 1280], P(('dp', 'tensor')), may hold values from -6 to 6
- gate_weights: float32 [32768, 2], P(('dp', 'tensor')), may hold values from 0.2 to 1
- routes: int32 [32768, 2], P(('dp', 'tensor')), may hold values from 0 to 31, as said below
- slot_index: int32 [32768, 2], P(('dp', 'tensor')), may hold values from -1 to 1, as said below
- qkv_weight: bfloat16 [1280, 16, 240], P(None, 'tensor'), may hold values from -0.15625 to 0.15625
- proj_weight: bfloat16 [16, 80, 1280], P('tensor'), may hold values from -1.25 to 1.25
- up_weight: bfloat16 [32, 1280, 5120], P('dp', None, 'tensor'), may hold values from -0.15625 to 0.15625
- down_weight: bfloat16 [32, 5120, 1280], P('dp', 'tensor'), may hold values from -0.078125 to 0.078125
Outputs:
- layer_out: bfloat16 [32768, 1280], P(('dp', 'tensor'))
- gate_grad: float32 [32768, 2], P(('dp', 'tensor'))
- grad_qkv: float32 [1280, 16, 240], P('dp', 'tensor')
- grad_proj: float32 [16, 80, 1280], P('tensor', None, 'dp')
- grad_up: bfloat16 [32, 1280, 5120], P('dp', None, 'tensor')
- grad_down: bfloat16 [32, 5120, 1280], P('dp', 'tensor')
Inputs may be any that keep to these rules, and one draw needn't show every extreme that they name: `routes`: the two experts of a row differ. `slot_index`: -1 marks a dropped pair; within the rows of one device (aligned blocks of 128 rows) and one expert, the kept pairs hold the slots 0, 1, 2, ... without gaps, each at most once.
All inputs are finite; a program needn't handle non-finite values.
Results may differ from a plain program's by a relative error of at most 0.035.
Values may be sent and summed in bfloat16 or wider, within the bound.
A program may use at most 128 MiB of HBM per device.

v0:
```python
from functools import partial
import math

import jax
import jax.numpy as jnp
from jax import lax
from jax.experimental import pallas as pl
from jax.experimental.pallas import tpu as pltpu
from jax.sharding import PartitionSpec as P

CAP = 2


MESH = pl.DeviceIdType.MESH
VM = pl.BlockSpec(memory_space=pltpu.VMEM)
DMA = pltpu.SemaphoreType.DMA
PIECES = 4
SIDE = 4


def ring_places():
    spot = lax.axis_index("tensor")
    return spot, lax.div(spot, 2), lax.rem(spot, 2)


def level_at(level, steps, count):
    return lax.rem(level + steps + count, count)


def ring_peers(count):
    spot, level, side = ring_places()
    return (
        level_at(level, 1, count) * 2 + side,
        level_at(level, -1, count) * 2 + side,
        level * 2 + 1 - side,
    )


def plane_peer(along_x, step):
    me = lax.axis_index("dp")
    x, y = lax.div(me, SIDE), lax.rem(me, SIDE)
    if along_x:
        return lax.rem(x + step + SIDE, SIDE) * SIDE + y
    return x * SIDE + lax.rem(y + step + SIDE, SIDE)


def signal(axis, peer):
    pl.semaphore_signal(
        pltpu.get_barrier_semaphore(), inc=1, device_id={axis: peer}, device_id_type=MESH
    )


def greet_ring(count):
    peers = ring_peers(count)
    for peer in peers:
        signal("tensor", peer)
    return len(peers)


def greet_plane():
    for along_x in (True, False):
        for step in range(1, SIDE):
            signal("dp", plane_peer(along_x, step))
    return 2 * (SIDE - 1)


def greet_groups():
    me = lax.axis_index("dp")
    count = lax.axis_size("dp")

    def call(step, carry):
        signal("dp", lax.rem(me + step, count))
        return carry

    lax.fori_loop(1, count, call, 0)
    return count - 1


def await_peers(total):
    pl.semaphore_wait(pltpu.get_barrier_semaphore(), total)


def remote(source, target, send, recv, axis, peer):
    return pltpu.make_async_remote_copy(
        src_ref=source,
        dst_ref=target,
        send_sem=send,
        recv_sem=recv,
        device_id={axis: peer},
        device_id_type=MESH,
    )


def travels(way, step, piece, last):
    return step != last or (piece < PIECES // 2) == (way == 0)


def block_at(ref, spot, piece):
    if len(ref.shape) == 3:
        size = ref.shape[1] // PIECES
        return ref.at[spot, pl.ds(piece * size, size)]
    per = PIECES // ref.shape[0]
    size = ref.shape[2] // per
    return ref.at[piece // per, spot, pl.ds(piece % per * size, size)]


def rows_at(ref, piece):
    size = ref.shape[0] // PIECES
    return ref.at[pl.ds(piece * size, size)]


class GatherRing:
    def __init__(self, own_ref, full_ref, send, recv, give, take, mine, count):
        self.spot, self.level, self.side = ring_places()
        self.peers = ring_peers(count)
        self.refs = (own_ref, full_ref, send, recv, give, take, mine)
        self.count, self.reach = count, count // 2
        self.left, self.moved = [], []

    def place(self, way, step):
        return level_at(self.level, -step if way == 0 else step, self.count)

    def hop(self, way, step, piece):
        own_ref, full_ref, send, recv = self.refs[:4]
        target = block_at(full_ref, self.place(way, step) * 2 + self.side, piece)
        source = rows_at(own_ref, piece) if step == 0 else target
        item = (way, step, piece)
        return remote(source, target, send.at[item], recv.at[item], "tensor", self.peers[way])

    def landed(self, way, step, piece):
        full_ref, send, recv = self.refs[1:4]
        target = block_at(full_ref, self.place(way, step + 1) * 2 + self.side, piece)
        item = (way, step, piece)
        return remote(target, target, send.at[item], recv.at[item], "tensor", self.peers[way])

    def across(self, way, step, piece, from_side):
        own_ref, full_ref, _, _, give, take, _ = self.refs
        target = block_at(full_ref, self.place(way, step) * 2 + from_side, piece)
        source = rows_at(own_ref, piece) if step == 0 else target
        item = (way, step, piece)
        return remote(source, target, give.at[item], take.at[item], "tensor", self.peers[2])

    def keep(self, piece):
        own_ref, full_ref, mine = self.refs[0], self.refs[1], self.refs[6]
        return pltpu.make_async_copy(
            rows_at(own_ref, piece), block_at(full_ref, self.spot, piece), mine.at[piece]
        )

    def begin(self):
        for piece in range(PIECES):
            for way in range(2):
                self.hop(way, 0, piece).start()
                self.left.append((way, 0, piece))
        for piece in range(PIECES):
            self.keep(piece).start()
            self.across(0, 0, piece, self.side).start()
            self.moved.append((0, 0, piece))

    def run(self, step):
        last = self.reach - 1
        for piece in range(PIECES):
            for way in range(2):
                if not travels(way, step, piece, last):
                    continue
                self.landed(way, step, piece).wait_recv()
                if step < last and travels(way, step + 1, piece, last):
                    self.hop(way, step + 1, piece).start()
                    self.left.append((way, step + 1, piece))
                self.across(way, step + 1, piece, self.side).start()
                self.moved.append((way, step + 1, piece))

    def finish(self):
        for piece in range(PIECES):
            self.keep(piece).wait()
        for item in self.left:
            self.hop(*item).wait_send()
        for item in self.moved:
            self.across(*item, self.side).wait_send()
            self.across(*item, 1 - self.side).wait_recv()


def gather_sems(count):
    reach = count // 2
    return [
        DMA((2, reach, PIECES)),
        DMA((2, reach, PIECES)),
        DMA((2, reach + 1, PIECES)),
        DMA((2, reach + 1, PIECES)),
        DMA((PIECES,)),
    ]


GATHER_SEMS = 5


def comm_call(kernel, out_shape, operands, scratch, ident):
    single = not isinstance(out_shape, list)
    return pl.pallas_call(
        kernel,
        out_shape=out_shape,
        in_specs=[VM] * len(operands),
        out_specs=VM if single else [VM] * len(out_shape),
        scratch_shapes=scratch,
        compiler_params=pltpu.CompilerParams(
            collective_id=ident, has_side_effects=True, vmem_limit_bytes=60 * 1024 * 1024
        ),
    )(*operands)


def gather_kernel(count, own_ref, full_ref, *sems):
    await_peers(greet_ring(count))
    ring = GatherRing(own_ref, full_ref, *sems, count)
    ring.begin()
    for step in range(count // 2):
        ring.run(step)
    ring.finish()


def gather_tensor(own, ident):
    spots = lax.axis_size("tensor")
    return comm_call(
        partial(gather_kernel, spots // 2),
        jax.ShapeDtypeStruct((spots,) + own.shape, own.dtype),
        [own],
        gather_sems(spots // 2),
        ident,
    )


class Swap:
    def __init__(self, along_x, source_ref, target_ref, send, recv, mine):
        me = lax.axis_index("dp")
        self.me = lax.div(me, SIDE) if along_x else lax.rem(me, SIDE)
        self.along_x = along_x
        self.refs = (source_ref, target_ref, send, recv)
        self.keep = pltpu.make_async_copy(
            self.block(source_ref, self.me), self.block(target_ref, self.me), mine
        )

    def block(self, ref, index):
        size = ref.shape[0] // SIDE
        return ref.at[pl.ds(pl.multiple_of(index * size, size), size)]

    def copy(self, step, outward):
        source_ref, target_ref, send, recv = self.refs
        there = lax.rem(self.me + (step if outward else SIDE - step), SIDE)
        return remote(
            self.block(source_ref, there),
            self.block(target_ref, self.me if outward else there),
            send.at[step],
            recv.at[step],
            "dp",
            plane_peer(self.along_x, step if outward else -step),
        )

    def start(self):
        for step in range(1, SIDE):
            self.copy(step, True).start()
        self.keep.start()

    def finish(self):
        self.keep.wait()
        for step in range(1, SIDE):
            self.copy(step, False).wait_recv()
        for step in range(1, SIDE):
            self.copy(step, True).wait_send()


def swap_sems():
    return [DMA((SIDE,)), DMA((SIDE,)), DMA(())]


def reorder(rows, kind):
    count = rows.shape[0]
    target = lax.broadcasted_iota(jnp.int32, (count, count), 0)
    source = lax.broadcasted_iota(jnp.int32, (count, count), 1)
    extents = {"x": SIDE, "y": SIDE, "e": count // (SIDE * SIDE * CAP), "c": CAP}

    def code(index, order):
        digits = {}
        for name in reversed(order):
            digits[name] = index % extents[name]
            index = index // extents[name]
        total = digits["x"]
        for name in "yec":
            total = total * extents[name] + digits[name]
        return total

    before, after = kind
    orders = {"x": "xyec", "y": "yexc", "e": "eyxc"}
    pick = (code(target, orders[after]) == code(source, orders[before])).astype(rows.dtype)
    return jnp.dot(pick, rows, preferred_element_type=jnp.float32).astype(rows.dtype)


class SlotsOut:
    def __init__(self, source_ref, first, second, third, done, sems):
        self.refs = (first, second, third, done)
        self.by_x = Swap(True, source_ref, first, *sems[:3])
        self.by_y = Swap(False, second, third, *sems[3:])

    def begin(self):
        self.by_x.start()

    def middle(self):
        first, second = self.refs[:2]
        self.by_x.finish()
        second[...] = reorder(first[...], "xy")
        self.by_y.start()

    def finish(self):
        third, done = self.refs[2:]
        self.by_y.finish()
        done[...] = reorder(third[...], "ye")


def out_scratch(slots):
    return [pltpu.VMEM(slots.shape, slots.dtype)] * 4 + swap_sems() + swap_sems()


OUT_SCRATCH = 10


def slots_kernel(count, source_ref, full_ref, *scratch):
    await_peers(greet_plane() + greet_ring(count))
    out = SlotsOut(source_ref, *scratch[:4], scratch[4:OUT_SCRATCH])
    out.begin()
    out.middle()
    out.finish()
    ring = GatherRing(scratch[3], full_ref, *scratch[OUT_SCRATCH:], count)
    ring.begin()
    for step in range(count // 2):
        ring.run(step)
    ring.finish()


def slots_shape(slots, local_experts):
    spots = lax.axis_size("tensor")
    rows, width = slots.shape
    return jax.ShapeDtypeStruct((local_experts, spots, rows // local_experts, width), slots.dtype)


def slots_out(slots, local_experts, ident):
    count = lax.axis_size("tensor") // 2
    return comm_call(
        partial(slots_kernel, count),
        slots_shape(slots, local_experts),
        [slots],
        out_scratch(slots) + gather_sems(count),
        ident,
    )


def opening_kernel(count, own_ref, source_ref, full_ref, slots_ref, *scratch):
    await_peers(greet_plane() + greet_ring(count))
    out = SlotsOut(source_ref, *scratch[:4], scratch[4:OUT_SCRATCH])
    sems = scratch[OUT_SCRATCH:]
    first = GatherRing(own_ref, full_ref, *sems[:GATHER_SEMS], count)
    second = GatherRing(scratch[3], slots_ref, *sems[GATHER_SEMS:], count)
    out.begin()
    first.begin()
    first.run(0)
    out.middle()
    first.run(1)
    out.finish()
    for step in range(2, count // 2):
        first.run(step)
    second.begin()
    first.finish()
    for step in range(count // 2):
        second.run(step)
    second.finish()


def opening(own, slots, local_experts, ident):
    spots = lax.axis_size("tensor")
    count = spots // 2
    return comm_call(
        partial(opening_kernel, count),
        [
            jax.ShapeDtypeStruct((spots,) + own.shape, own.dtype),
            slots_shape(slots, local_experts),
        ],
        [own, slots],
        out_scratch(slots) + gather_sems(count) + gather_sems(count),
        ident,
    )


class ReduceRing:
    def __init__(self, part_ref, total_ref, pair, stage, landing, send, recv, give, take, count):
        self.spot, self.level, self.side = ring_places()
        self.peers = ring_peers(count)
        self.part, self.total, self.pair = part_ref, total_ref, pair
        self.stage, self.landing = stage, landing
        self.sems = (send, recv, give, take)
        self.count, self.reach = count, count // 2
        self.plan = [
            (way, step, piece)
            for step in range(self.reach)
            for piece in range(PIECES)
            for way in range(2)
            if travels(way, step, piece, 0)
        ]
        self.own = [(0, self.reach, piece) for piece in range(PIECES)]

    def place(self, way, step):
        steps = self.reach - step
        return level_at(self.level, steps if way == 0 else -steps, self.count)

    def rows(self, way, step, piece):
        size = self.stage.shape[2] // PIECES
        return way, step, pl.ds(piece * size, size)

    def across(self, way, step, piece):
        there = self.place(way, step)
        item = (way, step, piece)
        return remote(
            block_at(self.part, there * 2 + 1 - self.side, piece),
            rows_at(self.pair.at[there], piece),
            self.sems[2].at[item],
            self.sems[3].at[item],
            "tensor",
            self.peers[2],
        )

    def hop(self, way, step, piece):
        item = (way, step, piece)
        where = self.rows(*item)
        return remote(
            self.stage.at[where],
            self.landing.at[where],
            self.sems[0].at[item],
            self.sems[1].at[item],
            "tensor",
            self.peers[way],
        )

    def local_sum(self, way, step, piece):
        there = self.place(way, step)
        self.across(way, step, piece).wait_recv()
        mine = block_at(self.part, there * 2 + self.side, piece)[...]
        return mine.astype(jnp.float32) + rows_at(self.pair.at[there], piece)[...].astype(
            jnp.float32
        )

    def arrived(self, way, step, piece):
        self.hop(way, step, piece).wait_recv()
        return self.landing[self.rows(way, step, piece)].astype(jnp.float32)

    def begin(self):
        for item in self.plan + self.own:
            self.across(*item).start()

    def run(self):
        for way, step, piece in self.plan:
            term = self.local_sum(way, step, piece)
            if step > 0 and travels(way, step - 1, piece, 0):
                term = term + self.arrived(way, step - 1, piece)
            self.stage[self.rows(way, step, piece)] = term.astype(self.stage.dtype)
            self.hop(way, step, piece).start()
        for way, step, piece in self.own:
            term = self.local_sum(way, step, piece)
            for side in range(2):
                term = term + self.arrived(side, self.reach - 1, piece)
            rows_at(self.total, piece)[...] = term.astype(self.total.dtype)

    def finish(self):
        for item in self.plan:
            self.hop(*item).wait_send()
        for item in self.plan + self.own:
            self.across(*item).wait_send()


def reduce_scratch(rows, width, dtype, count):
    reach = count // 2
    return [
        pltpu.VMEM((count, rows, width), dtype),
        pltpu.VMEM((2, reach, rows, width), dtype),
        pltpu.VMEM((2, reach, rows, width), dtype),
        DMA((2, reach, PIECES)),
        DMA((2, reach, PIECES)),
        DMA((2, reach + 1, PIECES)),
        DMA((2, reach + 1, PIECES)),
    ]


REDUCE_SCRATCH = 7


def reduce_kernel(count, part_ref, total_ref, *scratch):
    await_peers(greet_ring(count))
    ring = ReduceRing(part_ref, total_ref, *scratch, count)
    ring.begin()
    ring.run()
    ring.finish()


def reduce_tensor(part, ident):
    count = lax.axis_size("tensor") // 2
    _, rows, width = part.shape
    return comm_call(
        partial(reduce_kernel, count),
        jax.ShapeDtypeStruct((rows, width), jnp.float32),
        [part],
        reduce_scratch(rows, width, part.dtype, count),
        ident,
    )


class SlotsBack:
    def __init__(self, done, third, second, first, target_ref, sems):
        self.refs = (done, third, second, first)
        self.by_y = Swap(False, third, second, *sems[:3])
        self.by_x = Swap(True, first, target_ref, *sems[3:])

    def begin(self):
        done, third = self.refs[:2]
        third[...] = reorder(done[...], "ey")
        self.by_y.start()

    def middle(self):
        second, first = self.refs[2:]
        self.by_y.finish()
        first[...] = reorder(second[...], "yx")
        self.by_x.start()

    def finish(self):
        self.by_x.finish()


def back_kernel(count, parts, *refs):
    part_refs, refs = refs[:parts], refs[parts:]
    out_refs, refs = refs[:parts], refs[parts:]
    each = len(refs) // parts
    rings, backs = [], []
    for index in range(parts):
        mine = refs[index * each : (index + 1) * each]
        slots, ring = mine[:OUT_SCRATCH], mine[OUT_SCRATCH:]
        rings.append(ReduceRing(part_refs[index], slots[0], *ring, count))
        backs.append(SlotsBack(*slots[:4], out_refs[index], slots[4:]))
    await_peers(greet_plane() + greet_ring(count))
    for ring in rings:
        ring.begin()
    for ring, back in zip(rings, backs):
        ring.run()
        back.begin()
    for back in backs:
        back.middle()
    for back in backs:
        back.finish()
    for ring in rings:
        ring.finish()


def slots_back(part_list, ident):
    count = lax.axis_size("tensor") // 2
    scratch, shapes = [], []
    for part in part_list:
        experts, _, rows, width = part.shape
        slots = jax.ShapeDtypeStruct((experts * rows, width), part.dtype)
        shapes.append(slots)
        scratch += out_scratch(slots) + reduce_scratch(experts * rows, width, part.dtype, count)
    return comm_call(
        partial(back_kernel, count, len(part_list)), shapes, part_list, scratch, ident
    )


class Exchange:
    def __init__(self, source_ref, target_ref, send, recv, local_sem):
        self.me = lax.axis_index("dp")
        self.count = source_ref.shape[0]
        self.refs = (source_ref, target_ref, send, recv)
        self.keep = pltpu.make_async_copy(
            source_ref.at[self.me], target_ref.at[self.me], local_sem
        )

    def put(self, step):
        source_ref, target_ref, send, recv = self.refs
        peer = lax.rem(self.me + step, self.count)
        return remote(
            source_ref.at[peer], target_ref.at[self.me], send.at[step], recv.at[step], "dp", peer
        )

    def got(self, step):
        source_ref, target_ref, send, recv = self.refs
        peer = lax.rem(self.me - step + self.count, self.count)
        return remote(
            source_ref.at[peer], target_ref.at[peer], send.at[step], recv.at[step], "dp", peer
        )

    def start(self):
        def put_one(step, carry):
            self.put(step).start()
            return carry

        lax.fori_loop(1, self.count, put_one, 0)
        self.keep.start()

    def finish(self):
        self.keep.wait()

        def take_one(step, carry):
            self.got(step).wait_recv()
            self.put(step).wait_send()
            return carry

        lax.fori_loop(1, self.count, take_one, 0)


def exchange_sems(groups):
    return [DMA((groups,)), DMA((groups,)), DMA(())]


def groups_kernel(parts, *refs):
    part_refs, refs = refs[:parts], refs[parts:]
    out_refs, refs = refs[:parts], refs[parts:]
    await_peers(greet_groups())
    swaps = []
    for index in range(parts):
        landing, dsend, drecv, dlocal = refs[index * 4 : index * 4 + 4]
        swaps.append(Exchange(part_refs[index], landing, dsend, drecv, dlocal))
        swaps[-1].start()
    for index in range(parts):
        swaps[index].finish()
        landing = refs[index * 4]
        total = landing[0].astype(jnp.float32)
        for group in range(1, landing.shape[0]):
            total = total + landing[group].astype(jnp.float32)
        out_refs[index][...] = total


def reduce_groups(part_list, ident):
    scratch = []
    for part in part_list:
        scratch += [pltpu.VMEM(part.shape, part.dtype)] + exchange_sems(part.shape[0])
    return comm_call(
        partial(groups_kernel, len(part_list)),
        [jax.ShapeDtypeStruct(part.shape[1:], jnp.float32) for part in part_list],
        part_list,
        scratch,
        ident,
    )


epsilon = 1e-06
half_root = 1.0 / math.sqrt(2.0)
bell_scale = 1.0 / math.sqrt(2.0 * math.pi)


def norm_parts(row_block):
    widened = row_block.astype(jnp.float32)
    center = widened - jnp.mean(widened, axis=-1, keepdims=True)
    factor = lax.rsqrt(jnp.mean(center * center, axis=-1, keepdims=True) + epsilon)
    return (center * factor, factor)


def norm_back(normal_rows, factor, upstream):
    mean_up = jnp.mean(upstream, axis=-1, keepdims=True)
    mean_mix = jnp.mean(upstream * normal_rows, axis=-1, keepdims=True)
    return factor * (upstream - mean_up - normal_rows * mean_mix)


def gelu_value(pre_act):
    return 0.5 * pre_act * (1.0 + lax.erf(pre_act * half_root))


def gelu_slope(pre_act):
    return (
        0.5 * (1.0 + lax.erf(pre_act * half_root))
        + pre_act * jnp.exp(-0.5 * pre_act * pre_act) * bell_scale
    )


def block_shares(query_block, key_rows, score_scale):
    scores = (
        jnp.einsum("qk,tk->qt", query_block, key_rows, preferred_element_type=jnp.float32)
        * score_scale
    )
    raised = jnp.exp(scores)
    return raised / jnp.sum(raised, axis=-1, keepdims=True)


def attend_head(queries, key_rows, value_rows, block_rows, score_scale):
    block_count = queries.shape[0] // block_rows

    def attend_one_block(query_block):
        shares = block_shares(query_block, key_rows, score_scale)
        context = jnp.dot(
            shares.astype(jnp.bfloat16), value_rows, preferred_element_type=jnp.float32
        )
        return context.astype(jnp.bfloat16)

    outputs = lax.map(attend_one_block, queries.reshape(block_count, block_rows, queries.shape[1]))
    return outputs.reshape(queries.shape)


def head_backward(queries, key_rows, value_rows, grad_context, block_rows, score_scale):
    block_count = queries.shape[0] // block_rows

    def head_one_block(carry, pieces):
        grad_keys, grad_values = carry
        query_block, grad_block = pieces
        shares = block_shares(query_block, key_rows, score_scale)
        grad_shares = jnp.einsum(
            "qk,tk->qt", grad_block, value_rows, preferred_element_type=jnp.float32
        )
        grad_scores = (
            shares
            * (grad_shares - jnp.sum(shares * grad_shares, axis=-1, keepdims=True))
            * score_scale
        ).astype(jnp.bfloat16)
        grad_query = jnp.dot(grad_scores, key_rows, preferred_element_type=jnp.float32).astype(
            jnp.bfloat16
        )
        grad_keys = grad_keys + jnp.einsum(
            "qt,qk->tk", grad_scores, query_block, preferred_element_type=jnp.float32
        )
        grad_values = grad_values + jnp.einsum(
            "qt,qk->tk", shares.astype(jnp.bfloat16), grad_block, preferred_element_type=jnp.float32
        )
        return ((grad_keys, grad_values), grad_query)

    zeros_rows = jnp.zeros(key_rows.shape, jnp.float32)
    shaped = (
        queries.reshape(block_count, block_rows, queries.shape[1]),
        grad_context.reshape(block_count, block_rows, queries.shape[1]),
    )
    (grad_keys, grad_values), grad_queries = lax.scan(
        head_one_block, (zeros_rows, zeros_rows), shaped
    )
    return (
        grad_queries.reshape(queries.shape),
        grad_keys.astype(jnp.bfloat16),
        grad_values.astype(jnp.bfloat16),
    )


def shards(
    tokens,
    cotangent,
    gate_weights,
    routes,
    slot_index,
    qkv_weight,
    proj_weight,
    up_weight,
    down_weight,
):
    rows_dev, model_width = tokens.shape
    head_size = qkv_weight.shape[2] // 3
    score_scale = head_size ** (-0.5)
    group_count = lax.axis_size("dp")
    spots = lax.axis_size("tensor")
    local_experts = up_weight.shape[0]
    places = group_count * local_experts * CAP
    normal_in, factor_in = norm_parts(tokens)
    normed = normal_in.astype(jnp.bfloat16)
    slot_code = jnp.where(slot_index >= 0, routes * CAP + slot_index, -1)
    positions = jnp.arange(places, dtype=jnp.int32)
    pick_both = (slot_code[None, :, :] == positions[:, None, None]).astype(jnp.bfloat16)
    pick_first = pick_both[:, :, 0]
    pick_second = pick_both[:, :, 1]
    dispatch_rows = pick_first + pick_second
    upstream = cotangent.astype(jnp.float32)
    grad_first = (gate_weights[:, 0:1] * upstream).astype(jnp.bfloat16)
    grad_second = (gate_weights[:, 1:2] * upstream).astype(jnp.bfloat16)
    grad_outgoing = jnp.dot(pick_first, grad_first, preferred_element_type=jnp.float32) + jnp.dot(
        pick_second, grad_second, preferred_element_type=jnp.float32
    )
    full_norm, grad_arrived = opening(
        normed, grad_outgoing.astype(jnp.bfloat16), local_experts, 1
    )
    full_norm = full_norm.reshape(-1, model_width)
    grad_arrived = grad_arrived.reshape(local_experts, -1, model_width)
    seq_len = full_norm.shape[0]
    block_rows = min(512, seq_len)
    qkv_rows = jnp.einsum(
        "sd,dhc->hsc", full_norm, qkv_weight, preferred_element_type=jnp.float32
    ).astype(jnp.bfloat16)
    queries = qkv_rows[:, :, :head_size]
    key_rows = qkv_rows[:, :, head_size : 2 * head_size]
    value_rows = qkv_rows[:, :, 2 * head_size :]
    context = jax.vmap(partial(attend_head, block_rows=block_rows, score_scale=score_scale))(
        queries, key_rows, value_rows
    )
    attention = reduce_tensor(
        jnp.einsum("hsk,hkd->sd", context, proj_weight, preferred_element_type=jnp.float32)
        .astype(jnp.bfloat16)
        .reshape(spots, rows_dev, model_width),
        2,
    )
    mid = (tokens.astype(jnp.float32) + attention).astype(jnp.bfloat16)
    normal_mid, factor_mid = norm_parts(mid)
    mid_normed = normal_mid.astype(jnp.bfloat16)
    outgoing = jnp.dot(dispatch_rows, mid_normed, preferred_element_type=jnp.float32).astype(
        jnp.bfloat16
    )
    arrived = slots_out(outgoing, local_experts, 3).reshape(local_experts, -1, model_width)
    pre_act = jnp.einsum("end,edf->enf", arrived, up_weight, preferred_element_type=jnp.float32)
    hidden = gelu_value(pre_act).astype(jnp.bfloat16)
    expert_partial = jnp.einsum(
        "enf,efd->end", hidden, down_weight, preferred_element_type=jnp.float32
    )
    grad_hidden = jnp.einsum(
        "end,efd->enf", grad_arrived, down_weight, preferred_element_type=jnp.float32
    )
    grad_pre = (grad_hidden * gelu_slope(pre_act)).astype(jnp.bfloat16)
    grad_down = jnp.einsum(
        "enf,end->efd", hidden, grad_arrived, preferred_element_type=jnp.float32
    ).astype(jnp.bfloat16)
    grad_up = jnp.einsum(
        "end,enf->edf", arrived, grad_pre, preferred_element_type=jnp.float32
    ).astype(jnp.bfloat16)
    grad_partial = jnp.einsum(
        "enf,edf->end", grad_pre, up_weight, preferred_element_type=jnp.float32
    )
    grad_back, returned = slots_back(
        [
            part.astype(jnp.bfloat16).reshape(local_experts, spots, -1, model_width)
            for part in (grad_partial, expert_partial)
        ],
        5,
    )
    expert_first = jnp.einsum("pr,pd->rd", pick_first, returned, preferred_element_type=jnp.float32)
    expert_second = jnp.einsum(
        "pr,pd->rd", pick_second, returned, preferred_element_type=jnp.float32
    )
    mixed_rows = gate_weights[:, 0:1] * expert_first + gate_weights[:, 1:2] * expert_second
    layer_out = (mid.astype(jnp.float32) + mixed_rows).astype(jnp.bfloat16)
    gate_grad = jnp.stack(
        [jnp.sum(upstream * expert_first, axis=-1), jnp.sum(upstream * expert_second, axis=-1)],
        axis=1,
    )
    grad_norm = jnp.einsum(
        "pr,pd->rd", dispatch_rows, grad_back, preferred_element_type=jnp.float32
    )
    grad_mid = (upstream + norm_back(normal_mid, factor_mid, grad_norm)).astype(jnp.bfloat16)
    full_grad = gather_tensor(grad_mid, 6).reshape(-1, model_width)
    grad_context = jnp.einsum(
        "sd,hkd->hsk", full_grad, proj_weight, preferred_element_type=jnp.float32
    ).astype(jnp.bfloat16)
    grad_proj = jnp.einsum("hsk,sd->hdk", context, full_grad, preferred_element_type=jnp.float32)
    grad_queries, grad_keys, grad_values = jax.vmap(
        partial(head_backward, block_rows=block_rows, score_scale=score_scale)
    )(queries, key_rows, value_rows, grad_context)
    grad_rows = jnp.concatenate([grad_queries, grad_keys, grad_values], axis=-1)
    grad_qkv = jnp.einsum("sd,hsc->dhc", full_norm, grad_rows, preferred_element_type=jnp.float32)
    grad_qkv, grad_proj = reduce_groups(
        [
            grad_qkv.astype(jnp.bfloat16).reshape(group_count, -1, grad_qkv.shape[2]),
            grad_proj.astype(jnp.bfloat16).reshape(group_count, -1, head_size),
        ],
        7,
    )
    return (layer_out, gate_grad, grad_qkv[:, None, :], grad_proj.T[None], grad_up, grad_down)


def solution(mesh):
    return jax.shard_map(
        shards,
        mesh=mesh,
        in_specs=(
            P(("dp", "tensor"), None),
            P(("dp", "tensor"), None),
            P(("dp", "tensor"), None),
            P(("dp", "tensor"), None),
            P(("dp", "tensor"), None),
            P(None, "tensor", None),
            P("tensor", None, None),
            P("dp", None, "tensor"),
            P("dp", "tensor", None),
        ),
        out_specs=(
            P(("dp", "tensor"), None),
            P(("dp", "tensor"), None),
            P("dp", "tensor", None),
            P("tensor", None, "dp"),
            P("dp", None, "tensor"),
            P("dp", "tensor", None),
        ),
        check_vma=False,
    )
```

profile of v0, /device:TPU:2, one launch (start us, length us, event | category | flops | bytes accessed | tf_op | source)
XLA Modules:
  0.0 339.7 jit_solution(10261587888496699134)
XLA Ops:
  5.2 1.9 fusion.61.own_ref
  8.4 1.9 fusion.38.source_ref
  10.3 59.4 %shard_map.136 = (bf16[16,128,1280]{2,1,0:T(8,128)(2,1)}, bf16[2,16,32,1280]{3,2,1,0:T(8,128)(2,1)}) custom-call(bf16[128,1280]{1,0:T(8,128)(2,1)} %fusion.61.own_ref, bf16[64,1280]{1,0:T(8,128)(2,1)} %fusion.38.source_ref), custom_call_target="tpu_custom_call" | custom-call | tf_op jit(solution)/shard_map/pallas_call | solution.py:198
  69.8 4.0 %fusion.37 = bf16[1,2048,240]{1,2,0:T(8,128)(2,1)S(1)} fusion(bf16[2048,1280]{1,0:T(8,128)(2,1)} %bitcast.197, bf16[1280,1,240]{0,2,1:T(8,128)(2,1)S(1)} %copy-done.18), kind=kOutput, calls=%fused_computation.51 | convolution fusion | flops 1258782720 | bytes 6840320 | tf_op jit(solution)/shard_map/sd,dhc->hsc/dot_general | solution.py:777
  77.9 10.6 %while.25 = (s32[]{:T(128)}, bf16[4,1,512,80]{2,3,1,0:T(8,128)(2,1)}, bf16[4,1,512,80]{3,2,1,0:T(8,128)(2,1)S(1)}, bf16[1,2048,80]{2,1,0:T(8,128)(2,1)S(1)}, bf16[1,2048,80]{2,1,0:T(8,128)(2,1)}, /*index=5*/s32[]{:T(128)}) while((s32[]{:T(128)}, bf16[4,1,512,80]{2,3,1,0:T(8,128)(2,1)}, bf16[4,1,512,80]{3,2,1,0:T(8,128)(2,1)S(1)}, ...), condition=%wide.region_4.5_spmd, body=%wide.region_2.4_spmd.sunk | while | flops 340827648 | bytes 10768497 | solution.py:693
  79.0 1.6 fusion.128
  89.8 3.9 %convolution_convert_fusion.1 = bf16[2048,1280]{1,0:T(8,128)(2,1)} fusion(bf16[2048,80]{0,1:T(8,128)(2,1)S(1)} %bitcast.181, bf16[1,80,1280]{2,1,0:T(8,128)(2,1)S(1)} %copy-done.7), kind=kOutput, calls=%fused_computation.44 | convolution fusion | flops 422051840 | bytes 5775360 | tf_op jit(solution)/shard_map/hsk,hkd->sd/dot_general | solution.py:787
  93.7 35.1 %shard_map.137 = f32[128,1280]{1,0:T(8,128)} custom-call(bf16[16,128,1280]{2,1,0:T(8,128)(2,1)} %bitcast.177), custom_call_target="tpu_custom_call" | custom-call | tf_op jit(solution)/shard_map/pallas_call | solution.py:198
  131.8 31.2 %shard_map.138 = bf16[2,16,32,1280]{3,2,1,0:T(8,128)(2,1)} custom-call(bf16[64,1280]{1,0:T(8,128)(2,1)} %convolution_convert_fusion.10.source_ref), custom_call_target="tpu_custom_call" | custom-call | tf_op jit(solution)/shard_map/pallas_call | solution.py:198
  163.1 3.4 %fusion.91 = f32[2,512,320]{1,2,0:T(8,128)S(1)} fusion(bf16[2,512,1280]{2,1,0:T(8,128)(2,1)} %bitcast.179, bf16[2,1280,320]{1,2,0:T(8,128)(2,1)} %param.20), kind=kOutput, calls=%fused_computation.133 | convolution fusion | flops 838860800 | bytes 5570560 | tf_op jit(solution)/shard_map/end,edf->enf/dot_general | solution.py:799
  167.7 2.2 convolution_convert_fusion.5
  169.9 2.2 convolution_convert_fusion.4
  172.1 3.1 convolution_convert_fusion.2
  175.3 3.1 convolution_convert_fusion.3
  178.4 53.2 %shard_map.139 = (bf16[64,1280]{1,0:T(8,128)(2,1)}, bf16[64,1280]{1,0:T(8,128)(2,1)}) custom-call(bf16[2,16,32,1280]{3,2,1,0:T(8,128)(2,1)} %bitcast.186, bf16[2,16,32,1280]{3,2,1,0:T(8,128)(2,1)} %bitcast.185), custom_call_target="tpu_custom_call" | custom-call | tf_op jit(solution)/shard_map/pallas_call | solution.py:198
  234.1 2.4 fusion.66
  237.1 34.2 %shard_map.140 = bf16[16,128,1280]{2,1,0:T(8,128)(2,1)} custom-call(bf16[128,1280]{1,0:T(8,128)(2,1)} %get-tuple-element.200.own_ref), custom_call_target="tpu_custom_call" | custom-call | tf_op jit(solution)/shard_map/pallas_call | solution.py:198
  271.3 3.6 %convolution_convert_fusion.8 = bf16[1280,80]{0,1:T(8,128)(2,1)S(1)} fusion(bf16[2048,80]{0,1:T(8,128)(2,1)S(1)} %bitcast.182, bf16[2048,1280]{1,0:T(8,128)(2,1)} %bitcast.175), kind=kOutput, calls=%fused_computation.53 | convolution fusion | flops 419532800 | bytes 5775360 | tf_op jit(solution)/shard_map/hsk,sd->hdk/dot_general | solution.py:842
  275.3 2.4 fusion.39
  278.6 2.0 copy.40
  281.4 27.1 %while.26 = (s32[]{:T(128)}, f32[1,2048,80]{1,2,0:T(8,128)S(1)}, f32[1,2048,80]{1,2,0:T(8,128)}, bf16[4,1,512,80]{2,3,1,0:T(8,128)(2,1)}, bf16[4,1,512,80]{3,2,1...) while((s32[]{:T(128)}, f32[1,2048,80]{1,2,0:T(8,128)S(1)}, ...), condition=%wide.region_14.15_spmd.clone, body=%wide.region_11.14_spmd.clone.sunk | while | flops 855284736 | bytes 43938040 | solution.py:728
  310.7 3.9 %convolution_convert_fusion.6 = bf16[1280,240]{0,1:T(8,128)(2,1)S(1)} fusion(bf16[2048,1280]{1,0:T(8,128)(2,1)} %bitcast.198, bf16[1,2048,80]{1,2,0:T(8,128)(2,1)S(1)} %convert_element_type.147, bf16[1,2048,80]{1,2,0:T(8,128)(2,1)S(1)} %convert_element_type.146, bf16[1,2048,80]{1,2,0:T(8,128)(2,1)S(1)} %bitcast.192), kind=kOutput, calls=%fused_computation.49 | convolution fusion | flops 1261547520 | bytes 6840320 | tf_op jit(solution)/shard_map/sd,hsc->dhc/dot_general | solution.py:847
  315.7 21.0 %shard_map.141 = (f32[80,240]{1,0:T(8,128)}, f32[80,80]{1,0:T(8,128)}) custom-call(bf16[16,80,240]{2,1,0:T(8,128)(2,1)} %bitcast.187, bf16[16,80,80]{2,1,0:T(8,128)(2,1)} %bitcast.190), custom_call_target="tpu_custom_call" | custom-call | tf_op jit(solution)/shard_map/pallas_call | solution.py:198
  336.6 1.6 copy.38
  (133 shorter events, 61.1 us)
Async XLA Ops:
  0.6 165.8 %copy-start = (bf16[2,320,1280]{2,1,0:T(8,128)(2,1)S(1)}, bf16[2,320,1280]{2,1,0:T(8,128)(2,1)}, u32[]{:S(2)}) copy-start(bf16[2,320,1280]{2,1,0:T(8,128)(2,1)} %param.21) | copy-start | bytes 4915204
  0.6 69.1 %copy-start.18 = (bf16[1280,1,240]{0,2,1:T(8,128)(2,1)S(1)}, bf16[1280,1,240]{0,2,1:T(8,128)(2,1)}, u32[]{:S(2)}) copy-start(bf16[1280,1,240]{0,2,1:T(8,128)(2,1)} %param.18) | copy-start | bytes 1843204
  5.2 5.1 %copy-start.14 = (pred[64,128,2]{1,0,2:T(32,128)(4,1)}, pred[64,128,2]{1,0,2:T(32,128)(4,1)S(1)}, u32[]{:S(2)}) copy-start(pred[64,128,2]{1,0,2:T(32,128)(4,1)S(1)} %get-tuple-element.202) | copy-start | bytes 49156
  77.9 11.9 %copy-start.7 = (bf16[1,80,1280]{2,1,0:T(8,128)(2,1)S(1)}, bf16[1,80,1280]{2,1,0:T(8,128)(2,1)}, u32[]{:S(2)}) copy-start(bf16[1,80,1280]{2,1,0:T(8,128)(2,1)} %param.19) | copy-start | bytes 614404
  93.7 35.1 %copy-start.3 = (bf16[128,1280]{1,0:T(8,128)(2,1)S(1)}, bf16[128,1280]{1,0:T(8,128)(2,1)}, u32[]{:S(2)}) copy-start(bf16[128,1280]{1,0:T(8,128)(2,1)} %param.13) | copy-start | bytes 983044
  93.7 37.1 %copy-start.16 = (bf16[64,128,2]{1,0,2:T(8,128)(2,1)S(1)}, bf16[64,128,2]{1,0,2:T(8,128)(2,1)}, u32[]{:S(2)}) copy-start(bf16[64,128,2]{1,0,2:T(8,128)(2,1)} %get-tuple-element.201) | copy-start | bytes 98308
  163.1 3.4 %copy-start.6 = (bf16[2,16,32,1280]{3,2,1,0:T(8,128)(2,1)S(1)}, bf16[2,16,32,1280]{3,2,1,0:T(8,128)(2,1)}, u32[]{:S(2)}) copy-start(bf16[2,16,32,1280]{3,2,1,0:T(8,128)(2,1)} %get-tuple-element.85) | copy-start | bytes 7864324
  167.7 2.2 copy-start.2
  172.1 3.1 copy-start.17
  178.3 53.2 %copy-start.5 = (bf16[128,1280]{1,0:T(8,128)(2,1)S(1)}, bf16[128,1280]{1,0:T(8,128)(2,1)}, u32[]{:S(2)}) copy-start(bf16[128,1280]{1,0:T(8,128)(2,1)} %copy-done.4) | copy-start | bytes 983044
  178.3 54.6 %copy-start.15 = (pred[64,128,2]{1,0,2:T(32,128)(4,1)S(1)}, pred[64,128,2]{1,0,2:T(32,128)(4,1)}, u32[]{:S(2)}) copy-start(pred[64,128,2]{1,0,2:T(32,128)(4,1)} %copy-done.14) | copy-start | bytes 49156
  271.3 4.0 %copy-start.1 = (bf16[16,128,1280]{2,1,0:T(8,128)(2,1)S(1)}, bf16[16,128,1280]{2,1,0:T(8,128)(2,1)}, u32[]{:S(2)}) copy-start(bf16[16,128,1280]{2,1,0:T(8,128)(2,1)} %shard_map.140) | copy-start | bytes 15728644
  271.3 4.0 %copy-start.8 = (bf16[1,80,1280]{2,1,0:T(8,128)(2,1)S(1)}, bf16[1,80,1280]{2,1,0:T(8,128)(2,1)}, u32[]{:S(2)}) copy-start(bf16[1,80,1280]{2,1,0:T(8,128)(2,1)} %param.19) | copy-start | bytes 614404
  281.4 1.2 copy-start.13
  283.6 1.4 copy-start.10
  288.2 1.1 copy-start.9
  288.2 1.2 copy-start.13
  290.4 1.4 copy-start.10
  294.9 1.1 copy-start.9
  294.9 1.2 copy-start.13
  297.2 1.4 copy-start.10
  301.7 1.1 copy-start.9
  301.7 1.2 copy-start.13
  304.0 1.4 copy-start.10
  (10 other events, 10.2 us)
where the time goes:
time: 341 us; the launch traced here: 340 us
  Pallas kernels  234 us (69%)
  matrix products  72.5 us (21%)
  local copies, waits for them, and re-layouts  18.5 us (5%)
  other arithmetic  13.4 us (4%)
    pallas_call x6, Pallas kernels, comm_call(): pl.pallas_call(kernel, out_shape=out_shape, in_specs=[VM] * len(operands)...  234 us

commit v1 on v0

--- a/solution.py
+++ b/solution.py
@@ -640,6 +640,169 @@
         scratch,
         ident,
     )
+LANES = 128
+QUERY_BLOCK = 512
+KEY_BLOCK = 256
+
+
+def mm(left, right):
+    return jnp.dot(left, right, preferred_element_type=jnp.float32)
+
+
+def project_rows(norm_ref, weight_ref, rows_ref, cols_ref, index):
+    size = QUERY_BLOCK
+    rows = pl.ds(pl.multiple_of(index * size, size), size)
+    block = mm(norm_ref[rows, :], weight_ref[...])
+    rows_ref[rows, :] = block.astype(rows_ref.dtype)
+    cols_ref[:, rows] = block.T.astype(cols_ref.dtype)
+
+
+def attend_block(rows_ref, cols_ref, context_ref, inverse_ref, raised_ref, index, scale):
+    seq = rows_ref.shape[0]
+    here = pl.ds(pl.multiple_of(index * QUERY_BLOCK, QUERY_BLOCK), QUERY_BLOCK)
+    queries = cols_ref[0:LANES, here]
+    total = jnp.zeros((1, QUERY_BLOCK), jnp.float32)
+    for at in range(0, seq, KEY_BLOCK):
+        scores = mm(rows_ref[at : at + KEY_BLOCK, LANES : 2 * LANES], queries)
+        raised = jnp.exp(scores * scale)
+        raised_ref[at : at + KEY_BLOCK, :] = raised
+        total = total + jnp.sum(raised, axis=0, keepdims=True)
+    inverse = 1.0 / total
+    inverse_ref[:, here] = inverse
+    context = jnp.zeros((LANES, QUERY_BLOCK), jnp.float32)
+    for at in range(0, seq, KEY_BLOCK):
+        shares = (raised_ref[at : at + KEY_BLOCK, :] * inverse).astype(jnp.bfloat16)
+        context = context + mm(cols_ref[2 * LANES : 3 * LANES, at : at + KEY_BLOCK], shares)
+    context_ref[:, here] = context.astype(context_ref.dtype)
+
+
+def forward_kernel(scale, norm_ref, weight_ref, rows_ref, cols_ref, context_ref, inverse_ref, raised_ref):
+    blocks = norm_ref.shape[0] // QUERY_BLOCK
+
+    def project(index, carry):
+        project_rows(norm_ref, weight_ref, rows_ref, cols_ref, index)
+        return carry
+
+    def attend(index, carry):
+        attend_block(rows_ref, cols_ref, context_ref, inverse_ref, raised_ref, index, scale)
+        return carry
+
+    lax.fori_loop(0, blocks, project, 0)
+    lax.fori_loop(0, blocks, attend, 0)
+
+
+def attend_forward(full_norm, weight, scale):
+    seq = full_norm.shape[0]
+    return pl.pallas_call(
+        partial(forward_kernel, scale),
+        out_shape=[
+            jax.ShapeDtypeStruct((seq, 3 * LANES), jnp.bfloat16),
+            jax.ShapeDtypeStruct((3 * LANES, seq), jnp.bfloat16),
+            jax.ShapeDtypeStruct((LANES, seq), jnp.bfloat16),
+            jax.ShapeDtypeStruct((1, seq), jnp.float32),
+        ],
+        in_specs=[VM] * 2,
+        out_specs=[VM] * 4,
+        scratch_shapes=[pltpu.VMEM((seq, QUERY_BLOCK), jnp.float32)],
+        compiler_params=pltpu.CompilerParams(vmem_limit_bytes=60 * 1024 * 1024),
+    )(full_norm, weight)
+
+
+def backward_block(
+    rows_ref, cols_ref, context_ref, inverse_ref, grad_ref, proj_ref, gcols_ref, gkeys, gvals, index, scale
+):
+    seq = rows_ref.shape[0]
+    here = pl.ds(pl.multiple_of(index * QUERY_BLOCK, QUERY_BLOCK), QUERY_BLOCK)
+    queries = cols_ref[0:LANES, here]
+    query_rows = rows_ref[here, 0:LANES]
+    wide = lax.dot_general(
+        grad_ref[here, :],
+        proj_ref[...],
+        (((1,), (1,)), ((), ())),
+        preferred_element_type=jnp.float32,
+    )
+    grad_rows = wide.astype(jnp.bfloat16)
+    grad_cols = wide.T.astype(jnp.bfloat16)
+    inverse = inverse_ref[:, here]
+    delta = jnp.sum(
+        grad_cols.astype(jnp.float32) * context_ref[:, here].astype(jnp.float32),
+        axis=0,
+        keepdims=True,
+    )
+    grad_query = jnp.zeros((LANES, QUERY_BLOCK), jnp.float32)
+    for at in range(0, seq, KEY_BLOCK):
+        keys = slice(at, at + KEY_BLOCK)
+        scores = mm(rows_ref[keys, LANES : 2 * LANES], queries)
+        shares = jnp.exp(scores * scale) * inverse
+        grad_shares = mm(rows_ref[keys, 2 * LANES : 3 * LANES], grad_cols)
+        grad_scores = (shares * (grad_shares - delta)).astype(jnp.bfloat16)
+        gvals[keys, :] += mm(shares.astype(jnp.bfloat16), grad_rows)
+        gkeys[keys, :] += mm(grad_scores, query_rows)
+        grad_query = grad_query + mm(cols_ref[LANES : 2 * LANES, keys], grad_scores)
+    size = gcols_ref.shape[0] // 3
+    gcols_ref[0:size, here] = (grad_query[0:size] * scale).astype(gcols_ref.dtype)
+
+
+def backward_kernel(
+    scale,
+    norm_ref,
+    grad_ref,
+    proj_ref,
+    rows_ref,
+    cols_ref,
+    context_ref,
+    inverse_ref,
+    weights_ref,
+    gcols_ref,
+    gkeys,
+    gvals,
+):
+    seq = rows_ref.shape[0]
+    size = gcols_ref.shape[0] // 3
+    gkeys[...] = jnp.zeros_like(gkeys)
+    gvals[...] = jnp.zeros_like(gvals)
+
+    def one_block(index, carry):
+        backward_block(
+            rows_ref, cols_ref, context_ref, inverse_ref, grad_ref, proj_ref, gcols_ref, gkeys, gvals, index, scale
+        )
+        return carry
+
+    lax.fori_loop(0, seq // QUERY_BLOCK, one_block, 0)
+    for at in range(0, seq, QUERY_BLOCK):
+        there = slice(at, at + QUERY_BLOCK)
+        key_cols = (gkeys[there, :] * scale).T
+        value_cols = gvals[there, :].T
+        gcols_ref[size : 2 * size, there] = key_cols[0:size].astype(gcols_ref.dtype)
+        gcols_ref[2 * size : 3 * size, there] = value_cols[0:size].astype(gcols_ref.dtype)
+    step = norm_ref.shape[1] // 5
+    spare = jnp.zeros((3 * LANES - 4 * size, step), jnp.float32)
+
+    def weights(index, carry):
+        where = pl.ds(pl.multiple_of(index * step, step), step)
+        for_qkv = mm(gcols_ref[...], norm_ref[:, where])
+        for_proj = mm(context_ref[0:size, :], grad_ref[:, where])
+        block = jnp.concatenate([for_qkv, for_proj, spare], axis=0).T
+        weights_ref[where, :] = block[:, 0 : 4 * size].astype(weights_ref.dtype)
+        return carry
+
+    lax.fori_loop(0, 5, weights, 0)
+
+
+def attend_backward(full_norm, full_grad, proj, rows, cols, context, inverse, scale, size):
+    seq, width = full_norm.shape
+    return pl.pallas_call(
+        partial(backward_kernel, scale),
+        out_shape=jax.ShapeDtypeStruct((width, 4 * size), jnp.bfloat16),
+        in_specs=[VM] * 7,
+        out_specs=VM,
+        scratch_shapes=[
+            pltpu.VMEM((3 * size, seq), jnp.bfloat16),
+            pltpu.VMEM((seq, LANES), jnp.float32),
+            pltpu.VMEM((seq, LANES), jnp.float32),
+        ],
+        compiler_params=pltpu.CompilerParams(vmem_limit_bytes=60 * 1024 * 1024),
+    )(full_norm, full_grad, proj, rows, cols, context, inverse)
 
 
 epsilon = 1e-06
@@ -668,70 +831,6 @@
     return (
         0.5 * (1.0 + lax.erf(pre_act * half_root))
         + pre_act * jnp.exp(-0.5 * pre_act * pre_act) * bell_scale
-    )
-
-
-def block_shares(query_block, key_rows, score_scale):
-    scores = (
-        jnp.einsum("qk,tk->qt", query_block, key_rows, preferred_element_type=jnp.float32)
-        * score_scale
-    )
-    raised = jnp.exp(scores)
-    return raised / jnp.sum(raised, axis=-1, keepdims=True)
-
-
-def attend_head(queries, key_rows, value_rows, block_rows, score_scale):
-    block_count = queries.shape[0] // block_rows
-
-    def attend_one_block(query_block):
-        shares = block_shares(query_block, key_rows, score_scale)
-        context = jnp.dot(
-            shares.astype(jnp.bfloat16), value_rows, preferred_element_type=jnp.float32
-        )
-        return context.astype(jnp.bfloat16)
-
-    outputs = lax.map(attend_one_block, queries.reshape(block_count, block_rows, queries.shape[1]))
-    return outputs.reshape(queries.shape)
-
-
-def head_backward(queries, key_rows, value_rows, grad_context, block_rows, score_scale):
-    block_count = queries.shape[0] // block_rows
-
-    def head_one_block(carry, pieces):
-        grad_keys, grad_values = carry
-        query_block, grad_block = pieces
-        shares = block_shares(query_block, key_rows, score_scale)
-        grad_shares = jnp.einsum(
-            "qk,tk->qt", grad_block, value_rows, preferred_element_type=jnp.float32
-        )
-        grad_scores = (
-            shares
-            * (grad_shares - jnp.sum(shares * grad_shares, axis=-1, keepdims=True))
-            * score_scale
-        ).astype(jnp.bfloat16)
-        grad_query = jnp.dot(grad_scores, key_rows, preferred_element_type=jnp.float32).astype(
-            jnp.bfloat16
-        )
-        grad_keys = grad_keys + jnp.einsum(
-            "qt,qk->tk", grad_scores, query_block, preferred_element_type=jnp.float32
-        )
-        grad_values = grad_values + jnp.einsum(
-            "qt,qk->tk", shares.astype(jnp.bfloat16), grad_block, preferred_element_type=jnp.float32
-        )
-        return ((grad_keys, grad_values), grad_query)
-
-    zeros_rows = jnp.zeros(key_rows.shape, jnp.float32)
-    shaped = (
-        queries.reshape(block_count, block_rows, queries.shape[1]),
-        grad_context.reshape(block_count, block_rows, queries.shape[1]),
-    )
-    (grad_keys, grad_values), grad_queries = lax.scan(
-        head_one_block, (zeros_rows, zeros_rows), shaped
-    )
-    return (
-        grad_queries.reshape(queries.shape),
-        grad_keys.astype(jnp.bfloat16),
-        grad_values.astype(jnp.bfloat16),
     )
 
 
@@ -772,19 +871,13 @@
     )
     full_norm = full_norm.reshape(-1, model_width)
     grad_arrived = grad_arrived.reshape(local_experts, -1, model_width)
-    seq_len = full_norm.shape[0]
-    block_rows = min(512, seq_len)
-    qkv_rows = jnp.einsum(
-        "sd,dhc->hsc", full_norm, qkv_weight, preferred_element_type=jnp.float32
-    ).astype(jnp.bfloat16)
-    queries = qkv_rows[:, :, :head_size]
-    key_rows = qkv_rows[:, :, head_size : 2 * head_size]
-    value_rows = qkv_rows[:, :, 2 * head_size :]
-    context = jax.vmap(partial(attend_head, block_rows=block_rows, score_scale=score_scale))(
-        queries, key_rows, value_rows
-    )
+    pad = ((0, 0), (0, 0), (0, LANES - head_size))
+    wide_qkv = jnp.pad(qkv_weight.reshape(model_width, 3, head_size), pad)
+    wide_qkv = wide_qkv.reshape(model_width, 3 * LANES)
+    wide_proj = jnp.pad(proj_weight[0], ((0, LANES - head_size), (0, 0)))
+    qkv_rows, qkv_cols, context, inverse = attend_forward(full_norm, wide_qkv, score_scale)
     attention = reduce_tensor(
-        jnp.einsum("hsk,hkd->sd", context, proj_weight, preferred_element_type=jnp.float32)
+        jnp.einsum("ks,kd->sd", context, wide_proj, preferred_element_type=jnp.float32)
         .astype(jnp.bfloat16)
         .reshape(spots, rows_dev, model_width),
         2,
@@ -836,23 +929,24 @@
     )
     grad_mid = (upstream + norm_back(normal_mid, factor_mid, grad_norm)).astype(jnp.bfloat16)
     full_grad = gather_tensor(grad_mid, 6).reshape(-1, model_width)
-    grad_context = jnp.einsum(
-        "sd,hkd->hsk", full_grad, proj_weight, preferred_element_type=jnp.float32
-    ).astype(jnp.bfloat16)
-    grad_proj = jnp.einsum("hsk,sd->hdk", context, full_grad, preferred_element_type=jnp.float32)
-    grad_queries, grad_keys, grad_values = jax.vmap(
-        partial(head_backward, block_rows=block_rows, score_scale=score_scale)
-    )(queries, key_rows, value_rows, grad_context)
-    grad_rows = jnp.concatenate([grad_queries, grad_keys, grad_values], axis=-1)
-    grad_qkv = jnp.einsum("sd,hsc->dhc", full_norm, grad_rows, preferred_element_type=jnp.float32)
-    grad_qkv, grad_proj = reduce_groups(
-        [
-            grad_qkv.astype(jnp.bfloat16).reshape(group_count, -1, grad_qkv.shape[2]),
-            grad_proj.astype(jnp.bfloat16).reshape(group_count, -1, head_size),
-        ],
+    grad_weights = attend_backward(
+        full_norm,
+        full_grad,
+        wide_proj,
+        qkv_rows,
+        qkv_cols,
+        context,
+        inverse,
+        score_scale,
+        head_size,
+    )
+    (grad_weights,) = reduce_groups(
+        [grad_weights.reshape(group_count, -1, 4 * head_size)],
         7,
     )
-    return (layer_out, gate_grad, grad_qkv[:, None, :], grad_proj.T[None], grad_up, grad_down)
+    grad_qkv = grad_weights[:, None, : 3 * head_size]
+    grad_proj = grad_weights[:, 3 * head_size :].T[None]
+    return (layer_out, gate_grad, grad_qkv, grad_proj, grad_up, grad_down)
 
 
 def solution(mesh):

time: 341 us -> 314 us (0.921)
  matrix products: 72.5 us -> 26.7 us
  Pallas kernels: 234 us -> 272 us
  local copies, waits for them, and re-layouts: 18.5 us -> 6.21 us
  other arithmetic: 13.4 us -> 7.18 us
    dot_general x33 -> x1, matrix products: 48.3 us -> 4.96 us  [shards(): jnp.einsum('ks,kd->sd', context, wide_proj, preferred_element_type=jnp.fl...]
    pallas_call x0 -> x2, Pallas kernels: none -> 36.8 us  [the longest x1 24.7 us: attend_backward(): pl.pallas_call(partial(backward_kernel, scale), out_shape=jax.ShapeDtypeS...]
    while x44 -> x0, local copies, waits for them, and re-layouts: 6.45 us -> none  [the longest x4 3.76 us: attend_head(): lax.map(attend_one_block, queries.reshape(block_count, block_rows, querie...]
    convert_element_type x6 -> x0, other arithmetic: 5.57 us -> none  [the longest x4 4.41 us: head_one_block(): grad_scores = (shares * (grad_shares - jnp.sum(shares * grad_shares, axis...]
    unnamed x32 -> x20, local copies, waits for them, and re-layouts: 6.03 us -> 1.47 us
where the time goes in v1:
time: 314 us; the launch traced here: 313 us
  Pallas kernels  272 us (87%)
  matrix products  26.7 us (9%)
  other arithmetic  7.18 us (2%)
  local copies, waits for them, and re-layouts  6.21 us (2%)
    pallas_call x6, Pallas kernels, comm_call(): pl.pallas_call(kernel, out_shape=out_shape, in_specs=[VM] * len(operands)...  236 us
    pallas_call x1, Pallas kernels, attend_backward(): pl.pallas_call(partial(backward_kernel, scale), out_shape=jax.ShapeDtypeS...  24.7 us
    pallas_call x1, Pallas kernels, attend_forward(): pl.pallas_call(partial(forward_kernel, scale), out_shape=[jax.ShapeDtypeS...  12.1 us

profile of v1, /device:TPU:2, one launch (start us, length us, event | category | flops | bytes accessed | tf_op | source)
XLA Modules:
  0.0 313.4 jit_solution(15702664987422386966)
XLA Ops:
  0.7 1.2 convert_reduce_fusion.1
  1.9 1.2 fusion.17
  4.6 1.9 fusion.18.own_ref
  6.5 1.2 fusion.27
  9.6 1.3 copy.19.weight_ref
  10.9 59.4 %shard_map.136 = (bf16[16,128,1280]{2,1,0:T(8,128)(2,1)}, bf16[2,16,32,1280]{3,2,1,0:T(8,128)(2,1)}) custom-call(bf16[128,1280]{1,0:T(8,128)(2,1)} %fusion.18.own_ref, bf16[64,1280]{1,0:T(8,128)(2,1)} %fusion.source_ref), custom_call_target="tpu_custom_call" | custom-call | tf_op jit(solution)/shard_map/pallas_call | solution.py:198
  70.3 12.1 %shard_map.137 = (bf16[2048,384]{1,0:T(8,128)(2,1)}, bf16[384,2048]{1,0:T(8,128)(2,1)}, bf16[128,2048]{1,0:T(8,128)(2,1)}, f32[1,2048]{1,0:T(1,128)}) custom-call(bf16[2048,1280]{1,0:T(8,128)(2,1)} %bitcast.54, bf16[1280,384]{1,0:T(8,128)(2,1)} %copy.19.weight_ref), custom_call_target="tpu_custom_call" | custom-call | tf_op jit(solution)/shard_map/pallas_call | solution.py:696
  82.4 5.0 %convolution_convert_fusion = bf16[2048,1280]{1,0:T(8,128)(2,1)} fusion(bf16[128,2048]{1,0:T(8,128)(2,1)} %get-tuple-element.15.context_ref, bf16[80,1280]{1,0:T(8,128)(2,1)S(1)} %bitcast.66), kind=kOutput, calls=%fused_computation | convolution fusion | flops 673710080 | bytes 5971968 | tf_op jit(solution)/shard_map/ks,kd->sd/dot_general | solution.py:880
  87.4 35.1 %shard_map.138 = f32[128,1280]{1,0:T(8,128)} custom-call(bf16[16,128,1280]{2,1,0:T(8,128)(2,1)} %bitcast.53), custom_call_target="tpu_custom_call" | custom-call | tf_op jit(solution)/shard_map/pallas_call | solution.py:198
  122.5 1.2 convert_reduce_fusion
  125.0 31.2 %shard_map.139 = bf16[2,16,32,1280]{3,2,1,0:T(8,128)(2,1)} custom-call(bf16[64,1280]{1,0:T(8,128)(2,1)} %convolution_convert_fusion.5.source_ref), custom_call_target="tpu_custom_call" | custom-call | tf_op jit(solution)/shard_map/pallas_call | solution.py:198
  156.3 2.9 fusion.45
  159.2 1.2 fusion.1
  160.4 2.2 convolution_convert_fusion.4
  162.6 2.2 convolution_convert_fusion.3
  164.8 3.1 %convolution_convert_fusion.1 = bf16[2,512,1280]{2,1,0:T(8,128)(2,1)} fusion(bf16[2,320,1280]{2,1,0:T(8,128)(2,1)S(1)} %copy-done, f32[2,512,320]{1,2,0:T(8,128)S(1)} %fusion.45), kind=kOutput, calls=%fused_computation.1 | convolution fusion | flops 841809920 | bytes 5570560 | tf_op jit(solution)/shard_map/enf,efd->end/dot_general | solution.py:894
  168.0 3.1 convolution_convert_fusion.2
  171.0 53.2 %shard_map.140 = (bf16[64,1280]{1,0:T(8,128)(2,1)}, bf16[64,1280]{1,0:T(8,128)(2,1)}) custom-call(bf16[2,16,32,1280]{3,2,1,0:T(8,128)(2,1)} %bitcast.64, bf16[2,16,32,1280]{3,2,1,0:T(8,128)(2,1)} %bitcast.63), custom_call_target="tpu_custom_call" | custom-call | tf_op jit(solution)/shard_map/pallas_call | solution.py:198
  224.2 1.3 fusion.43
  225.6 1.2 fusion.35
  226.8 1.3 fusion.23
  228.7 34.2 %shard_map.141 = bf16[16,128,1280]{2,1,0:T(8,128)(2,1)} custom-call(bf16[128,1280]{1,0:T(8,128)(2,1)} %get-tuple-element.41.own_ref), custom_call_target="tpu_custom_call" | custom-call | tf_op jit(solution)/shard_map/pallas_call | solution.py:198
  262.9 24.7 %shard_map.142 = bf16[1280,320]{1,0:T(8,128)(2,1)} custom-call(bf16[2048,1280]{1,0:T(8,128)(2,1)} %bitcast.55, bf16[2048,1280]{1,0:T(8,128)(2,1)} %bitcast.56, bf16[128,1280]{1,0:T(8,128)(2,1)} %pad.9.proj_ref, bf16[2048,384]{1,0:T(8,128)(2,1)} %get-tuple-element.19.rows_ref, bf16[384,2048]{1,0:T(8,128)(2,1)} %get-tuple-element.20.cols_ref, ...), custom_call_target="tpu_custom_call" | custom-call | tf_op jit(solution)/shard_map/pallas_call | solution.py:794
  287.6 22.5 %shard_map.143 = f32[80,320]{1,0:T(8,128)} custom-call(bf16[16,80,320]{2,1,0:T(8,128)(2,1)} %bitcast.59), custom_call_target="tpu_custom_call" | custom-call | tf_op jit(solution)/shard_map/pallas_call | solution.py:198
  (36 shorter events, 8.4 us)
Async XLA Ops:
  0.6 158.6 %copy-start = (bf16[2,320,1280]{2,1,0:T(8,128)(2,1)S(1)}, bf16[2,320,1280]{2,1,0:T(8,128)(2,1)}, u32[]{:S(2)}) copy-start(bf16[2,320,1280]{2,1,0:T(8,128)(2,1)} %param.17) | copy-start | bytes 4915204
  0.6 7.2 %copy-start.4 = (bf16[128,1280]{1,0:T(8,128)(2,1)S(1)}, bf16[128,1280]{1,0:T(8,128)(2,1)}, u32[]{:S(2)}) copy-start(bf16[128,1280]{1,0:T(8,128)(2,1)} %param.10) | copy-start | bytes 983044
  0.7 8.1 %copy-start.5 = (bf16[1,80,1280]{2,1,0:T(8,128)(2,1)S(1)}, bf16[1,80,1280]{2,1,0:T(8,128)(2,1)}, u32[]{:S(2)}) copy-start(bf16[1,80,1280]{2,1,0:T(8,128)(2,1)} %param.15) | copy-start | bytes 614404
  0.7 8.8 %copy-start.6 = (bf16[1280,1,240]{0,2,1:T(8,128)(2,1)S(1)}, bf16[1280,1,240]{0,2,1:T(8,128)(2,1)}, u32[]{:S(2)}) copy-start(bf16[1280,1,240]{0,2,1:T(8,128)(2,1)} %param.14) | copy-start | bytes 1843204
  87.4 35.1 %copy-start.2 = (bf16[128,1280]{1,0:T(8,128)(2,1)S(1)}, bf16[128,1280]{1,0:T(8,128)(2,1)}, u32[]{:S(2)}) copy-start(bf16[128,1280]{1,0:T(8,128)(2,1)} %param.9) | copy-start | bytes 983044
  124.0 32.2 %copy-start.8 = (bf16[2,1280,320]{1,2,0:T(8,128)(2,1)S(1)}, bf16[2,1280,320]{1,2,0:T(8,128)(2,1)}, u32[]{:S(2)}) copy-start(bf16[2,1280,320]{1,2,0:T(8,128)(2,1)} %param.16) | copy-start | bytes 4915204
  156.2 3.0 copy-start.3
  160.4 2.2 copy-start.1
  224.2 2.6 copy-start.7

commit v2 on v1

--- a/solution.py
+++ b/solution.py
@@ -115,7 +115,7 @@
         self.peers = ring_peers(count)
         self.refs = (own_ref, full_ref, send, recv, give, take, mine)
         self.count, self.reach = count, count // 2
-        self.left, self.moved = [], []
+        self.left, self.moved, self.settled = [], [], []
 
     def place(self, way, step):
         return level_at(self.level, -step if way == 0 else step, self.count)
@@ -169,14 +169,21 @@
                 self.across(way, step + 1, piece, self.side).start()
                 self.moved.append((way, step + 1, piece))
 
+    def settle(self, way, step):
+        for item in [item for item in self.moved if item[:2] == (way, step)]:
+            if step == 0:
+                self.keep(item[2]).wait()
+            self.across(*item, 1 - self.side).wait_recv()
+            self.settled.append(item)
+
     def finish(self):
-        for piece in range(PIECES):
-            self.keep(piece).wait()
+        for way, step in [(0, 0)] + [(way, step) for step in range(1, self.reach + 1) for way in range(2)]:
+            if not any(item[:2] == (way, step) for item in self.settled):
+                self.settle(way, step)
         for item in self.left:
             self.hop(*item).wait_send()
         for item in self.moved:
             self.across(*item, self.side).wait_send()
-            self.across(*item, 1 - self.side).wait_recv()
 
 
 def gather_sems(count):
@@ -205,26 +212,6 @@
             collective_id=ident, has_side_effects=True, vmem_limit_bytes=60 * 1024 * 1024
         ),
     )(*operands)
-
-
-def gather_kernel(count, own_ref, full_ref, *sems):
-    await_peers(greet_ring(count))
-    ring = GatherRing(own_ref, full_ref, *sems, count)
-    ring.begin()
-    for step in range(count // 2):
-        ring.run(step)
-    ring.finish()
-
-
-def gather_tensor(own, ident):
-    spots = lax.axis_size("tensor")
-    return comm_call(
-        partial(gather_kernel, spots // 2),
-        jax.ShapeDtypeStruct((spots,) + own.shape, own.dtype),
-        [own],
-        gather_sems(spots // 2),
-        ident,
-    )
 
 
 class Swap:
@@ -451,18 +438,27 @@
         for item in self.plan + self.own:
             self.across(*item).start()
 
-    def run(self):
+    def run_step(self, at):
         for way, step, piece in self.plan:
+            if step != at:
+                continue
             term = self.local_sum(way, step, piece)
             if step > 0 and travels(way, step - 1, piece, 0):
                 term = term + self.arrived(way, step - 1, piece)
             self.stage[self.rows(way, step, piece)] = term.astype(self.stage.dtype)
             self.hop(way, step, piece).start()
+
+    def close(self):
         for way, step, piece in self.own:
             term = self.local_sum(way, step, piece)
             for side in range(2):
                 term = term + self.arrived(side, self.reach - 1, piece)
             rows_at(self.total, piece)[...] = term.astype(self.total.dtype)
+
+    def run(self):
+        for step in range(self.reach):
+            self.run_step(step)
+        self.close()
 
     def finish(self):
         for item in self.plan:
@@ -568,24 +564,29 @@
 class Exchange:
     def __init__(self, source_ref, target_ref, send, recv, local_sem):
         self.me = lax.axis_index("dp")
-        self.count = source_ref.shape[0]
+        self.count = target_ref.shape[0]
         self.refs = (source_ref, target_ref, send, recv)
         self.keep = pltpu.make_async_copy(
-            source_ref.at[self.me], target_ref.at[self.me], local_sem
+            self.block(self.me), target_ref.at[self.me], local_sem
         )
 
+    def block(self, index):
+        source_ref, target_ref = self.refs[:2]
+        size = target_ref.shape[1]
+        return source_ref.at[pl.ds(pl.multiple_of(index * size, size), size)]
+
     def put(self, step):
-        source_ref, target_ref, send, recv = self.refs
+        target_ref, send, recv = self.refs[1:]
         peer = lax.rem(self.me + step, self.count)
         return remote(
-            source_ref.at[peer], target_ref.at[self.me], send.at[step], recv.at[step], "dp", peer
+            self.block(peer), target_ref.at[self.me], send.at[step], recv.at[step], "dp", peer
         )
 
     def got(self, step):
-        source_ref, target_ref, send, recv = self.refs
+        target_ref, send, recv = self.refs[1:]
         peer = lax.rem(self.me - step + self.count, self.count)
         return remote(
-            source_ref.at[peer], target_ref.at[peer], send.at[step], recv.at[step], "dp", peer
+            self.block(peer), target_ref.at[peer], send.at[step], recv.at[step], "dp", peer
         )
 
     def start(self):
@@ -609,40 +610,10 @@
 
 def exchange_sems(groups):
     return [DMA((groups,)), DMA((groups,)), DMA(())]
-
-
-def groups_kernel(parts, *refs):
-    part_refs, refs = refs[:parts], refs[parts:]
-    out_refs, refs = refs[:parts], refs[parts:]
-    await_peers(greet_groups())
-    swaps = []
-    for index in range(parts):
-        landing, dsend, drecv, dlocal = refs[index * 4 : index * 4 + 4]
-        swaps.append(Exchange(part_refs[index], landing, dsend, drecv, dlocal))
-        swaps[-1].start()
-    for index in range(parts):
-        swaps[index].finish()
-        landing = refs[index * 4]
-        total = landing[0].astype(jnp.float32)
-        for group in range(1, landing.shape[0]):
-            total = total + landing[group].astype(jnp.float32)
-        out_refs[index][...] = total
-
-
-def reduce_groups(part_list, ident):
-    scratch = []
-    for part in part_list:
-        scratch += [pltpu.VMEM(part.shape, part.dtype)] + exchange_sems(part.shape[0])
-    return comm_call(
-        partial(groups_kernel, len(part_list)),
-        [jax.ShapeDtypeStruct(part.shape[1:], jnp.float32) for part in part_list],
-        part_list,
-        scratch,
-        ident,
-    )
 LANES = 128
 QUERY_BLOCK = 512
 KEY_BLOCK = 256
+BACK_KEYS = 512
 
 
 def mm(left, right):
@@ -709,14 +680,16 @@
 
 
 def backward_block(
-    rows_ref, cols_ref, context_ref, inverse_ref, grad_ref, proj_ref, gcols_ref, gkeys, gvals, index, scale
+    rows_ref, cols_ref, context_ref, inverse_ref, grad_ref, proj_ref, gcols_ref, gkeys, gvals, level, scale
 ):
     seq = rows_ref.shape[0]
-    here = pl.ds(pl.multiple_of(index * QUERY_BLOCK, QUERY_BLOCK), QUERY_BLOCK)
+    size = gcols_ref.shape[0] // 3
+    block = 2 * grad_ref.shape[1]
+    here = pl.ds(pl.multiple_of(level * block, block), block)
     queries = cols_ref[0:LANES, here]
     query_rows = rows_ref[here, 0:LANES]
     wide = lax.dot_general(
-        grad_ref[here, :],
+        grad_ref[pl.ds(level * 2, 2)].reshape(block, grad_ref.shape[2]),
         proj_ref[...],
         (((1,), (1,)), ((), ())),
         preferred_element_type=jnp.float32,
@@ -729,9 +702,9 @@
         axis=0,
         keepdims=True,
     )
-    grad_query = jnp.zeros((LANES, QUERY_BLOCK), jnp.float32)
-    for at in range(0, seq, KEY_BLOCK):
-        keys = slice(at, at + KEY_BLOCK)
+    grad_query = jnp.zeros((LANES, block), jnp.float32)
+    for at in range(0, seq, BACK_KEYS):
+        keys = slice(at, at + BACK_KEYS)
         scores = mm(rows_ref[keys, LANES : 2 * LANES], queries)
         shares = jnp.exp(scores * scale) * inverse
         grad_shares = mm(rows_ref[keys, 2 * LANES : 3 * LANES], grad_cols)
@@ -739,70 +712,142 @@
         gvals[keys, :] += mm(shares.astype(jnp.bfloat16), grad_rows)
         gkeys[keys, :] += mm(grad_scores, query_rows)
         grad_query = grad_query + mm(cols_ref[LANES : 2 * LANES, keys], grad_scores)
+    gcols_ref[0:size, here] = (grad_query[0:size] * scale).astype(gcols_ref.dtype)
+
+
+def flip_sums(gcols_ref, gkeys, gvals, scale):
     size = gcols_ref.shape[0] // 3
-    gcols_ref[0:size, here] = (grad_query[0:size] * scale).astype(gcols_ref.dtype)
-
-
-def backward_kernel(
+    for at in range(0, gkeys.shape[0], QUERY_BLOCK):
+        there = slice(at, at + QUERY_BLOCK)
+        key_cols = (gkeys[there, :] * scale).T
+        value_cols = gvals[there, :].T
+        gcols_ref[size : 2 * size, there] = key_cols[0:size].astype(gcols_ref.dtype)
+        gcols_ref[2 * size : 3 * size, there] = value_cols[0:size].astype(gcols_ref.dtype)
+
+
+def weight_sums(norm_ref, grad_ref, context_ref, gcols_ref, weights_ref, first, last):
+    size = gcols_ref.shape[0] // 3
+    step = 2 * LANES
+    spare = jnp.zeros((3 * LANES - 4 * size, step), jnp.float32)
+
+    def one(index, carry):
+        where = pl.ds(pl.multiple_of(index * step, step), step)
+        for_qkv = mm(gcols_ref[...], norm_ref[:, where])
+        rows = grad_ref[:, :, where].reshape(norm_ref.shape[0], step)
+        for_proj = mm(context_ref[0:size, :], rows)
+        block = jnp.concatenate([for_qkv, for_proj, spare], axis=0).T
+        weights_ref[where, :] = block[:, 0 : 4 * size].astype(weights_ref.dtype)
+        return carry
+
+    lax.fori_loop(first, last, one, 0)
+
+
+def closing_kernel(
+    count,
     scale,
+    own_ref,
+    part_ref,
     norm_ref,
-    grad_ref,
     proj_ref,
     rows_ref,
     cols_ref,
     context_ref,
     inverse_ref,
-    weights_ref,
+    slots_ref,
+    sum_ref,
+    grad_ref,
     gcols_ref,
     gkeys,
     gvals,
+    weights_ref,
+    landing,
+    *refs,
 ):
-    seq = rows_ref.shape[0]
-    size = gcols_ref.shape[0] // 3
+    ring_sems, refs = refs[:GATHER_SEMS], refs[GATHER_SEMS:]
+    swap_refs, refs = refs[:3], refs[3:]
+    slots, reduce = refs[:OUT_SCRATCH], refs[OUT_SCRATCH:]
+    _, level, _ = ring_places()
+    ring = GatherRing(own_ref, grad_ref, *ring_sems, count)
+    back_ring = ReduceRing(part_ref, slots[0], *reduce, count)
+    back = SlotsBack(*slots[:4], slots_ref, slots[4:])
+    swap = Exchange(weights_ref, landing, *swap_refs)
+    total = greet_groups() + greet_ring(count)
     gkeys[...] = jnp.zeros_like(gkeys)
     gvals[...] = jnp.zeros_like(gvals)
-
-    def one_block(index, carry):
+    await_peers(total)
+
+    def block(level):
         backward_block(
-            rows_ref, cols_ref, context_ref, inverse_ref, grad_ref, proj_ref, gcols_ref, gkeys, gvals, index, scale
+            rows_ref, cols_ref, context_ref, inverse_ref, grad_ref, proj_ref, gcols_ref, gkeys, gvals, level, scale
         )
-        return carry
-
-    lax.fori_loop(0, seq // QUERY_BLOCK, one_block, 0)
-    for at in range(0, seq, QUERY_BLOCK):
-        there = slice(at, at + QUERY_BLOCK)
-        key_cols = (gkeys[there, :] * scale).T
-        value_cols = gvals[there, :].T
-        gcols_ref[size : 2 * size, there] = key_cols[0:size].astype(gcols_ref.dtype)
-        gcols_ref[2 * size : 3 * size, there] = value_cols[0:size].astype(gcols_ref.dtype)
-    step = norm_ref.shape[1] // 5
-    spare = jnp.zeros((3 * LANES - 4 * size, step), jnp.float32)
-
-    def weights(index, carry):
-        where = pl.ds(pl.multiple_of(index * step, step), step)
-        for_qkv = mm(gcols_ref[...], norm_ref[:, where])
-        for_proj = mm(context_ref[0:size, :], grad_ref[:, where])
-        block = jnp.concatenate([for_qkv, for_proj, spare], axis=0).T
-        weights_ref[where, :] = block[:, 0 : 4 * size].astype(weights_ref.dtype)
-        return carry
-
-    lax.fori_loop(0, 5, weights, 0)
-
-
-def attend_backward(full_norm, full_grad, proj, rows, cols, context, inverse, scale, size):
-    seq, width = full_norm.shape
-    return pl.pallas_call(
-        partial(backward_kernel, scale),
-        out_shape=jax.ShapeDtypeStruct((width, 4 * size), jnp.bfloat16),
-        in_specs=[VM] * 7,
-        out_specs=VM,
-        scratch_shapes=[
+
+    reach = count // 2
+    ring.begin()
+    ring.settle(0, 0)
+    block(level)
+    back_ring.begin()
+
+    for step in range(reach):
+        ring.run(step)
+        for way in range(2):
+            ring.settle(way, step + 1)
+        if step < reach - 1:
+
+            def one_way(way, carry, step=step):
+                away = (2 * way - 1) * (step + 1)
+                block(level_at(level, away, count))
+                return carry
+
+            lax.fori_loop(0, 2, one_way, 0)
+        else:
+            back_ring.run_step(0)
+            block(level_at(level, reach, count))
+    flip_sums(gcols_ref, gkeys, gvals, scale)
+    back_ring.run_step(1)
+    parts = norm_ref.shape[1] // (2 * LANES)
+    weight_sums(norm_ref, grad_ref, context_ref, gcols_ref, weights_ref, 0, parts // 2)
+    back_ring.run_step(2)
+    weight_sums(norm_ref, grad_ref, context_ref, gcols_ref, weights_ref, parts // 2, parts)
+    swap.start()
+    back_ring.run_step(3)
+    back_ring.close()
+    back.begin()
+    back.middle()
+    swap.finish()
+    sums = landing[0].astype(jnp.float32)
+    for group in range(1, landing.shape[0]):
+        sums = sums + landing[group].astype(jnp.float32)
+    sum_ref[...] = sums
+    back.finish()
+    ring.finish()
+    back_ring.finish()
+
+
+def closing(own, part, norm, proj, rows, cols, context, inverse, scale, size, ident):
+    spots = lax.axis_size("tensor")
+    count = spots // 2
+    groups = lax.axis_size("dp")
+    seq, width = norm.shape
+    experts, _, slot_rows, _ = part.shape
+    slots = jax.ShapeDtypeStruct((experts * slot_rows, width), part.dtype)
+    return comm_call(
+        partial(closing_kernel, count, scale),
+        [slots, jax.ShapeDtypeStruct((width // groups, 4 * size), jnp.float32)],
+        [own, part, norm, proj, rows, cols, context, inverse],
+        [
+            pltpu.VMEM((spots,) + own.shape, own.dtype),
             pltpu.VMEM((3 * size, seq), jnp.bfloat16),
             pltpu.VMEM((seq, LANES), jnp.float32),
             pltpu.VMEM((seq, LANES), jnp.float32),
-        ],
-        compiler_params=pltpu.CompilerParams(vmem_limit_bytes=60 * 1024 * 1024),
-    )(full_norm, full_grad, proj, rows, cols, context, inverse)
+            pltpu.VMEM((width, 4 * size), jnp.bfloat16),
+            pltpu.VMEM((groups, width // groups, 4 * size), jnp.bfloat16),
+        ]
+        + gather_sems(count)
+        + exchange_sems(groups)
+        + out_scratch(slots)
+        + reduce_scratch(experts * slot_rows, width, part.dtype, count),
+        ident,
+    )
 
 
 epsilon = 1e-06
@@ -907,31 +952,19 @@
     grad_partial = jnp.einsum(
         "enf,edf->end", grad_pre, up_weight, preferred_element_type=jnp.float32
     )
-    grad_back, returned = slots_back(
-        [
-            part.astype(jnp.bfloat16).reshape(local_experts, spots, -1, model_width)
-            for part in (grad_partial, expert_partial)
-        ],
-        5,
-    )
-    expert_first = jnp.einsum("pr,pd->rd", pick_first, returned, preferred_element_type=jnp.float32)
-    expert_second = jnp.einsum(
-        "pr,pd->rd", pick_second, returned, preferred_element_type=jnp.float32
-    )
-    mixed_rows = gate_weights[:, 0:1] * expert_first + gate_weights[:, 1:2] * expert_second
-    layer_out = (mid.astype(jnp.float32) + mixed_rows).astype(jnp.bfloat16)
-    gate_grad = jnp.stack(
-        [jnp.sum(upstream * expert_first, axis=-1), jnp.sum(upstream * expert_second, axis=-1)],
-        axis=1,
-    )
+    grad_partial, expert_partial = (
+        part.astype(jnp.bfloat16).reshape(local_experts, spots, -1, model_width)
+        for part in (grad_partial, expert_partial)
+    )
+    (grad_back,) = slots_back([grad_partial], 5)
     grad_norm = jnp.einsum(
         "pr,pd->rd", dispatch_rows, grad_back, preferred_element_type=jnp.float32
     )
     grad_mid = (upstream + norm_back(normal_mid, factor_mid, grad_norm)).astype(jnp.bfloat16)
-    full_grad = gather_tensor(grad_mid, 6).reshape(-1, model_width)
-    grad_weights = attend_backward(
+    returned, grad_weights = closing(
+        grad_mid,
+        expert_partial,
         full_norm,
-        full_grad,
         wide_proj,
         qkv_rows,
         qkv_cols,
@@ -939,10 +972,17 @@
         inverse,
         score_scale,
         head_size,
-    )
-    (grad_weights,) = reduce_groups(
-        [grad_weights.reshape(group_count, -1, 4 * head_size)],
-        7,
+        6,
+    )
+    expert_first = jnp.einsum("pr,pd->rd", pick_first, returned, preferred_element_type=jnp.float32)
+    expert_second = jnp.einsum(
+        "pr,pd->rd", pick_second, returned, preferred_element_type=jnp.float32
+    )
+    mixed_rows = gate_weights[:, 0:1] * expert_first + gate_weights[:, 1:2] * expert_second
+    layer_out = (mid.astype(jnp.float32) + mixed_rows).astype(jnp.bfloat16)
+    gate_grad = jnp.stack(
+        [jnp.sum(upstream * expert_first, axis=-1), jnp.sum(upstream * expert_second, axis=-1)],
+        axis=1,
     )
     grad_qkv = grad_weights[:, None, : 3 * head_size]
     grad_proj = grad_weights[:, 3 * head_size :].T[None]

time: 314 us -> 284 us (0.904)
  Pallas kernels: 272 us -> 242 us
    pallas_call x1 -> x0, Pallas kernels: 24.7 us -> none  [attend_backward(): pl.pallas_call(partial(backward_kernel, scale), out_shape=jax.ShapeDtypeS...]
    pallas_call x6 -> x5, Pallas kernels: 236 us -> 230 us  [comm_call(): pl.pallas_call(kernel, out_shape=out_shape, in_specs=[VM] * len(operands)...]
where the time goes in v2:
time: 284 us; the launch traced here: 283 us
  Pallas kernels  242 us (85%)
  matrix products  28.6 us (10%)
  local copies, waits for them, and re-layouts  6.05 us (2%)
  other arithmetic  5.31 us (2%)
    pallas_call x5, Pallas kernels, comm_call(): pl.pallas_call(kernel, out_shape=out_shape, in_specs=[VM] * len(operands)...  230 us
    pallas_call x1, Pallas kernels, attend_forward(): pl.pallas_call(partial(forward_kernel, scale), out_shape=[jax.ShapeDtypeS...  12.1 us

profile of v2, /device:TPU:2, one launch (start us, length us, event | category | flops | bytes accessed | tf_op | source)
XLA Modules:
  0.0 282.8 jit_solution(7061062506188284874)
XLA Ops:
  2.3 1.2 fusion.27
  3.5 1.9 fusion.source_ref
  5.8 0.9 fusion.18.own_ref
  6.8 59.3 %shard_map.136 = (bf16[16,128,1280]{2,1,0:T(8,128)(2,1)}, bf16[2,16,32,1280]{3,2,1,0:T(8,128)(2,1)}) custom-call(bf16[128,1280]{1,0:T(8,128)(2,1)} %fusion.18.own_ref, bf16[64,1280]{1,0:T(8,128)(2,1)} %fusion.source_ref), custom_call_target="tpu_custom_call" | custom-call | tf_op jit(solution)/shard_map/pallas_call | solution.py:205
  66.1 1.1 pad.8
  67.3 1.3 copy.19.weight_ref
  68.6 12.1 %shard_map.137 = (bf16[2048,384]{1,0:T(8,128)(2,1)}, bf16[384,2048]{1,0:T(8,128)(2,1)}, bf16[128,2048]{1,0:T(8,128)(2,1)}, f32[1,2048]{1,0:T(1,128)}) custom-call(bf16[2048,1280]{1,0:T(8,128)(2,1)} %bitcast.52, bf16[1280,384]{1,0:T(8,128)(2,1)} %copy.19.weight_ref), custom_call_target="tpu_custom_call" | custom-call | tf_op jit(solution)/shard_map/pallas_call | solution.py:667
  80.7 5.0 %convolution_convert_fusion = bf16[2048,1280]{1,0:T(8,128)(2,1)} fusion(bf16[128,2048]{1,0:T(8,128)(2,1)} %get-tuple-element.15.context_ref, bf16[80,1280]{1,0:T(8,128)(2,1)S(1)} %bitcast.61), kind=kOutput, calls=%fused_computation | convolution fusion | flops 673710080 | bytes 5971968 | tf_op jit(solution)/shard_map/ks,kd->sd/dot_general | solution.py:925
  85.7 35.3 %shard_map.138 = f32[128,1280]{1,0:T(8,128)} custom-call(bf16[16,128,1280]{2,1,0:T(8,128)(2,1)} %bitcast.51), custom_call_target="tpu_custom_call" | custom-call | tf_op jit(solution)/shard_map/pallas_call | solution.py:205
  121.0 1.2 convert_reduce_fusion
  122.5 1.0 convolution_convert_fusion.5.source_ref
  123.4 31.1 %shard_map.139 = bf16[2,16,32,1280]{3,2,1,0:T(8,128)(2,1)} custom-call(bf16[64,1280]{1,0:T(8,128)(2,1)} %convolution_convert_fusion.5.source_ref), custom_call_target="tpu_custom_call" | custom-call | tf_op jit(solution)/shard_map/pallas_call | solution.py:205
  154.6 2.9 %fusion.45 = f32[2,512,320]{1,2,0:T(8,128)S(1)} fusion(bf16[2,512,1280]{2,1,0:T(8,128)(2,1)} %bitcast.54, bf16[2,1280,320]{1,2,0:T(8,128)(2,1)S(1)} %copy-done), kind=kOutput, calls=%fused_computation.77 | convolution fusion | flops 838860800 | bytes 5570560 | tf_op jit(solution)/shard_map/end,edf->enf/dot_general | solution.py:937
  157.6 1.2 fusion.1
  159.4 2.2 convolution_convert_fusion.3
  161.5 2.2 convolution_convert_fusion.4
  163.8 3.1 %convolution_convert_fusion.2 = bf16[2,512,1280]{2,1,0:T(8,128)(2,1)} fusion(bf16[2,512,320]{1,2,0:T(8,128)(2,1)S(1)} %fusion.1, bf16[2,1280,320]{1,2,0:T(8,128)(2,1)S(1)} %copy-done), kind=kOutput, calls=%fused_computation.2 | convolution fusion | flops 840171520 | bytes 4915200 | tf_op jit(solution)/shard_map/enf,edf->end/dot_general | solution.py:952
  166.8 33.2 %shard_map.140 = bf16[64,1280]{1,0:T(8,128)(2,1)} custom-call(bf16[2,16,32,1280]{3,2,1,0:T(8,128)(2,1)} %bitcast.59), custom_call_target="tpu_custom_call" | custom-call | tf_op jit(solution)/shard_map/pallas_call | solution.py:205
  200.1 1.4 fusion.43
  201.5 1.0 fusion.23.own_ref
  202.6 3.1 %convolution_convert_fusion.1 = bf16[2,512,1280]{2,1,0:T(8,128)(2,1)} fusion(bf16[2,320,1280]{2,1,0:T(8,128)(2,1)S(1)} %copy-done.8, f32[2,512,320]{1,2,0:T(8,128)S(1)} %fusion.45), kind=kOutput, calls=%fused_computation.1 | convolution fusion | flops 841809920 | bytes 5570560 | tf_op jit(solution)/shard_map/enf,efd->end/dot_general | solution.py:939
  206.4 70.9 %shard_map.141 = (bf16[64,1280]{1,0:T(8,128)(2,1)}, f32[80,320]{1,0:T(8,128)}) custom-call(bf16[128,1280]{1,0:T(8,128)(2,1)} %fusion.23.own_ref, bf16[2,16,32,1280]{3,2,1,0:T(8,128)(2,1)} %bitcast.60, bf16[2048,1280]{1,0:T(8,128)(2,1)} %bitcast.53, bf16[128,1280]{1,0:T(8,128)(2,1)} %pad.9.proj_ref, bf16[2048,384]{1,0:T(8,128)(2,1)} %get-tuple-element.17.rows_ref, ...), custom_call_target="tpu_custom_call" | custom-call | tf_op jit(solution)/shard_map/pallas_call | solution.py:205
  277.4 1.2 fusion.35
  278.6 2.1 fusion.24
  (35 shorter events, 5.7 us)
Async XLA Ops:
  0.6 154.0 %copy-start = (bf16[2,1280,320]{1,2,0:T(8,128)(2,1)S(1)}, bf16[2,1280,320]{1,2,0:T(8,128)(2,1)}, u32[]{:S(2)}) copy-start(bf16[2,1280,320]{1,2,0:T(8,128)(2,1)} %param.16) | copy-start | bytes 4915204
  0.6 4.8 %copy-start.2 = (bf16[128,1280]{1,0:T(8,128)(2,1)S(1)}, bf16[128,1280]{1,0:T(8,128)(2,1)}, u32[]{:S(2)}) copy-start(bf16[128,1280]{1,0:T(8,128)(2,1)} %param.9) | copy-start | bytes 983044
  68.6 12.1 %copy-start.5 = (bf16[1,80,1280]{2,1,0:T(8,128)(2,1)S(1)}, bf16[1,80,1280]{2,1,0:T(8,128)(2,1)}, u32[]{:S(2)}) copy-start(bf16[1,80,1280]{2,1,0:T(8,128)(2,1)} %param.15) | copy-start | bytes 614404
  154.6 3.0 %copy-start.4 = (bf16[2,16,32,1280]{3,2,1,0:T(8,128)(2,1)S(1)}, bf16[2,16,32,1280]{3,2,1,0:T(8,128)(2,1)}, u32[]{:S(2)}) copy-start(bf16[2,16,32,1280]{3,2,1,0:T(8,128)(2,1)} %get-tuple-element.16) | copy-start | bytes 7864324
  154.6 3.0 %copy-start.7 = (bf16[2,320,1280]{2,1,0:T(8,128)(2,1)S(1)}, bf16[2,320,1280]{2,1,0:T(8,128)(2,1)}, u32[]{:S(2)}) copy-start(bf16[2,320,1280]{2,1,0:T(8,128)(2,1)} %param.17) | copy-start | bytes 4915204
  157.6 1.7 copy-start.1
  166.8 34.7 %copy-start.3 = (bf16[128,1280]{1,0:T(8,128)(2,1)S(1)}, bf16[128,1280]{1,0:T(8,128)(2,1)}, u32[]{:S(2)}) copy-start(bf16[128,1280]{1,0:T(8,128)(2,1)} %param.10) | copy-start | bytes 983044
  200.1 2.5 copy-start.8
  277.4 3.9 %copy-start.6 = (f32[80,320]{1,0:T(8,128)S(1)}, f32[80,320]{1,0:T(8,128)}, u32[]{:S(2)}) copy-start(f32[80,320]{1,0:T(8,128)} %get-tuple-element.21) | copy-start | bytes 307204

commit v3 on v2

--- a/solution.py
+++ b/solution.py
@@ -307,70 +307,10 @@
 OUT_SCRATCH = 10
 
 
-def slots_kernel(count, source_ref, full_ref, *scratch):
-    await_peers(greet_plane() + greet_ring(count))
-    out = SlotsOut(source_ref, *scratch[:4], scratch[4:OUT_SCRATCH])
-    out.begin()
-    out.middle()
-    out.finish()
-    ring = GatherRing(scratch[3], full_ref, *scratch[OUT_SCRATCH:], count)
-    ring.begin()
-    for step in range(count // 2):
-        ring.run(step)
-    ring.finish()
-
-
 def slots_shape(slots, local_experts):
     spots = lax.axis_size("tensor")
     rows, width = slots.shape
     return jax.ShapeDtypeStruct((local_experts, spots, rows // local_experts, width), slots.dtype)
-
-
-def slots_out(slots, local_experts, ident):
-    count = lax.axis_size("tensor") // 2
-    return comm_call(
-        partial(slots_kernel, count),
-        slots_shape(slots, local_experts),
-        [slots],
-        out_scratch(slots) + gather_sems(count),
-        ident,
-    )
-
-
-def opening_kernel(count, own_ref, source_ref, full_ref, slots_ref, *scratch):
-    await_peers(greet_plane() + greet_ring(count))
-    out = SlotsOut(source_ref, *scratch[:4], scratch[4:OUT_SCRATCH])
-    sems = scratch[OUT_SCRATCH:]
-    first = GatherRing(own_ref, full_ref, *sems[:GATHER_SEMS], count)
-    second = GatherRing(scratch[3], slots_ref, *sems[GATHER_SEMS:], count)
-    out.begin()
-    first.begin()
-    first.run(0)
-    out.middle()
-    first.run(1)
-    out.finish()
-    for step in range(2, count // 2):
-        first.run(step)
-    second.begin()
-    first.finish()
-    for step in range(count // 2):
-        second.run(step)
-    second.finish()
-
-
-def opening(own, slots, local_experts, ident):
-    spots = lax.axis_size("tensor")
-    count = spots // 2
-    return comm_call(
-        partial(opening_kernel, count),
-        [
-            jax.ShapeDtypeStruct((spots,) + own.shape, own.dtype),
-            slots_shape(slots, local_experts),
-        ],
-        [own, slots],
-        out_scratch(slots) + gather_sems(count) + gather_sems(count),
-        ident,
-    )
 
 
 class ReduceRing:
@@ -434,9 +374,14 @@
         self.hop(way, step, piece).wait_recv()
         return self.landing[self.rows(way, step, piece)].astype(jnp.float32)
 
+    def begin_step(self, at):
+        for item in self.plan + self.own:
+            if item[1] == at:
+                self.across(*item).start()
+
     def begin(self):
-        for item in self.plan + self.own:
-            self.across(*item).start()
+        for step in range(self.reach + 1):
+            self.begin_step(step)
 
     def run_step(self, at):
         for way, step, piece in self.plan:
@@ -481,26 +426,6 @@
 
 
 REDUCE_SCRATCH = 7
-
-
-def reduce_kernel(count, part_ref, total_ref, *scratch):
-    await_peers(greet_ring(count))
-    ring = ReduceRing(part_ref, total_ref, *scratch, count)
-    ring.begin()
-    ring.run()
-    ring.finish()
-
-
-def reduce_tensor(part, ident):
-    count = lax.axis_size("tensor") // 2
-    _, rows, width = part.shape
-    return comm_call(
-        partial(reduce_kernel, count),
-        jax.ShapeDtypeStruct((rows, width), jnp.float32),
-        [part],
-        reduce_scratch(rows, width, part.dtype, count),
-        ident,
-    )
 
 
 class SlotsBack:
@@ -620,15 +545,18 @@
     return jnp.dot(left, right, preferred_element_type=jnp.float32)
 
 
-def project_rows(norm_ref, weight_ref, rows_ref, cols_ref, index):
-    size = QUERY_BLOCK
-    rows = pl.ds(pl.multiple_of(index * size, size), size)
-    block = mm(norm_ref[rows, :], weight_ref[...])
+def project_rows(norm_ref, weight_ref, rows_ref, cols_ref, level):
+    size = 2 * norm_ref.shape[1]
+    rows = pl.ds(pl.multiple_of(level * size, size), size)
+    taken = norm_ref[pl.ds(level * 2, 2)].reshape(size, norm_ref.shape[2])
+    block = mm(taken, weight_ref[...])
     rows_ref[rows, :] = block.astype(rows_ref.dtype)
     cols_ref[:, rows] = block.T.astype(cols_ref.dtype)
 
 
-def attend_block(rows_ref, cols_ref, context_ref, inverse_ref, raised_ref, index, scale):
+def attend_block(
+    rows_ref, cols_ref, context_ref, inverse_ref, raised_ref, context_rows, index, scale
+):
     seq = rows_ref.shape[0]
     here = pl.ds(pl.multiple_of(index * QUERY_BLOCK, QUERY_BLOCK), QUERY_BLOCK)
     queries = cols_ref[0:LANES, here]
@@ -645,38 +573,157 @@
         shares = (raised_ref[at : at + KEY_BLOCK, :] * inverse).astype(jnp.bfloat16)
         context = context + mm(cols_ref[2 * LANES : 3 * LANES, at : at + KEY_BLOCK], shares)
     context_ref[:, here] = context.astype(context_ref.dtype)
-
-
-def forward_kernel(scale, norm_ref, weight_ref, rows_ref, cols_ref, context_ref, inverse_ref, raised_ref):
-    blocks = norm_ref.shape[0] // QUERY_BLOCK
-
-    def project(index, carry):
-        project_rows(norm_ref, weight_ref, rows_ref, cols_ref, index)
+    context_rows[here, :] = context.T.astype(context_rows.dtype)
+
+
+def front_kernel(
+    count,
+    scale,
+    own_ref,
+    source_ref,
+    tokens_ref,
+    dispatch_ref,
+    weight_ref,
+    proj_ref,
+    norm_ref,
+    gslots_ref,
+    rows_ref,
+    cols_ref,
+    context_ref,
+    inverse_ref,
+    mid_ref,
+    arrived_ref,
+    raised_ref,
+    context_rows,
+    part_ref,
+    total_ref,
+    outgoing_ref,
+    *refs,
+):
+    _, level, _ = ring_places()
+    reach = count // 2
+    grads, refs = refs[:OUT_SCRATCH], refs[OUT_SCRATCH:]
+    slots, refs = refs[:OUT_SCRATCH], refs[OUT_SCRATCH:]
+    sems, refs = refs[: 3 * GATHER_SEMS], refs[3 * GATHER_SEMS :]
+    grads_out = SlotsOut(source_ref, *grads[:4], grads[4:])
+    slots_out = SlotsOut(outgoing_ref, *slots[:4], slots[4:])
+    first = GatherRing(own_ref, norm_ref, *sems[:GATHER_SEMS], count)
+    second = GatherRing(grads[3], gslots_ref, *sems[GATHER_SEMS : 2 * GATHER_SEMS], count)
+    third = GatherRing(slots[3], arrived_ref, *sems[2 * GATHER_SEMS :], count)
+    reduce = ReduceRing(part_ref, total_ref, *refs, count)
+    await_peers(greet_plane() + greet_ring(count))
+
+    def both_ways(act, distance):
+        def one_way(way, carry):
+            act(level_at(level, (2 * way - 1) * distance, count))
+            return carry
+
+        lax.fori_loop(0, 2, one_way, 0)
+
+    def project(place):
+        project_rows(norm_ref, weight_ref, rows_ref, cols_ref, place)
+
+    def attend(index, carry):
+        attend_block(
+            rows_ref, cols_ref, context_ref, inverse_ref, raised_ref, context_rows, index, scale
+        )
         return carry
 
-    def attend(index, carry):
-        attend_block(rows_ref, cols_ref, context_ref, inverse_ref, raised_ref, index, scale)
-        return carry
-
-    lax.fori_loop(0, blocks, project, 0)
-    lax.fori_loop(0, blocks, attend, 0)
-
-
-def attend_forward(full_norm, weight, scale):
-    seq = full_norm.shape[0]
-    return pl.pallas_call(
-        partial(forward_kernel, scale),
-        out_shape=[
+    def fill_part(place):
+        size = 2 * part_ref.shape[1]
+        rows = pl.ds(pl.multiple_of(place * size, size), size)
+        block = mm(context_rows[rows, :], proj_ref[...]).astype(part_ref.dtype)
+        part_ref[pl.ds(place * 2, 2)] = block.reshape(2, part_ref.shape[1], part_ref.shape[2])
+
+    grads_out.begin()
+    first.begin()
+    first.settle(0, 0)
+    project(level)
+    for step in range(reach):
+        first.run(step)
+        if step == 0:
+            grads_out.middle()
+        if step == 1:
+            grads_out.finish()
+        if step == reach - 1:
+            second.begin()
+        for way in range(2):
+            first.settle(way, step + 1)
+        if step < reach - 1:
+            both_ways(project, step + 1)
+        else:
+            project(level_at(level, reach, count))
+    blocks = norm_ref.shape[0] * norm_ref.shape[1] // QUERY_BLOCK
+    lax.fori_loop(0, blocks // 2, attend, 0)
+    second.run(0)
+    second.run(1)
+    lax.fori_loop(blocks // 2, blocks, attend, 0)
+    second.run(2)
+    fill_part(level_at(level, reach, count))
+    reduce.begin_step(0)
+    both_ways(fill_part, reach - 1)
+    reduce.begin_step(1)
+    second.run(3)
+    reduce.run_step(0)
+    both_ways(fill_part, reach - 2)
+    reduce.begin_step(2)
+    reduce.run_step(1)
+    both_ways(fill_part, reach - 3)
+    reduce.begin_step(3)
+    fill_part(level)
+    reduce.begin_step(reach)
+    reduce.run_step(2)
+    reduce.run_step(3)
+    first.finish()
+    second.finish()
+    reduce.close()
+    mid = (tokens_ref[...].astype(jnp.float32) + total_ref[...]).astype(mid_ref.dtype)
+    mid_ref[...] = mid
+    normal, _ = norm_parts(mid)
+    outgoing_ref[...] = mm(dispatch_ref[...], normal.astype(jnp.bfloat16)).astype(
+        outgoing_ref.dtype
+    )
+    slots_out.begin()
+    slots_out.middle()
+    slots_out.finish()
+    third.begin()
+    for step in range(reach):
+        third.run(step)
+    third.finish()
+    reduce.finish()
+
+
+def front(own, grad_slots, tokens, dispatch, weight, proj, scale, local_experts, ident):
+    spots = lax.axis_size("tensor")
+    count = spots // 2
+    rows, width = own.shape
+    seq = spots * rows
+    return comm_call(
+        partial(front_kernel, count, scale),
+        [
+            jax.ShapeDtypeStruct((spots,) + own.shape, own.dtype),
+            slots_shape(grad_slots, local_experts),
             jax.ShapeDtypeStruct((seq, 3 * LANES), jnp.bfloat16),
             jax.ShapeDtypeStruct((3 * LANES, seq), jnp.bfloat16),
             jax.ShapeDtypeStruct((LANES, seq), jnp.bfloat16),
             jax.ShapeDtypeStruct((1, seq), jnp.float32),
+            jax.ShapeDtypeStruct(tokens.shape, tokens.dtype),
+            slots_shape(grad_slots, local_experts),
         ],
-        in_specs=[VM] * 2,
-        out_specs=[VM] * 4,
-        scratch_shapes=[pltpu.VMEM((seq, QUERY_BLOCK), jnp.float32)],
-        compiler_params=pltpu.CompilerParams(vmem_limit_bytes=60 * 1024 * 1024),
-    )(full_norm, weight)
+        [own, grad_slots, tokens, dispatch, weight, proj],
+        [
+            pltpu.VMEM((seq, QUERY_BLOCK), jnp.float32),
+            pltpu.VMEM((seq, LANES), jnp.bfloat16),
+            pltpu.VMEM((spots, rows, width), jnp.bfloat16),
+            pltpu.VMEM((rows, width), jnp.float32),
+            pltpu.VMEM(grad_slots.shape, grad_slots.dtype),
+        ]
+        + out_scratch(grad_slots)
+        + out_scratch(grad_slots)
+        + gather_sems(count) * 3
+        + reduce_scratch(rows, width, jnp.bfloat16, count),
+        ident,
+    )
 
 
 def backward_block(
@@ -911,29 +958,25 @@
     grad_outgoing = jnp.dot(pick_first, grad_first, preferred_element_type=jnp.float32) + jnp.dot(
         pick_second, grad_second, preferred_element_type=jnp.float32
     )
-    full_norm, grad_arrived = opening(
-        normed, grad_outgoing.astype(jnp.bfloat16), local_experts, 1
-    )
-    full_norm = full_norm.reshape(-1, model_width)
-    grad_arrived = grad_arrived.reshape(local_experts, -1, model_width)
     pad = ((0, 0), (0, 0), (0, LANES - head_size))
     wide_qkv = jnp.pad(qkv_weight.reshape(model_width, 3, head_size), pad)
     wide_qkv = wide_qkv.reshape(model_width, 3 * LANES)
     wide_proj = jnp.pad(proj_weight[0], ((0, LANES - head_size), (0, 0)))
-    qkv_rows, qkv_cols, context, inverse = attend_forward(full_norm, wide_qkv, score_scale)
-    attention = reduce_tensor(
-        jnp.einsum("ks,kd->sd", context, wide_proj, preferred_element_type=jnp.float32)
-        .astype(jnp.bfloat16)
-        .reshape(spots, rows_dev, model_width),
-        2,
-    )
-    mid = (tokens.astype(jnp.float32) + attention).astype(jnp.bfloat16)
+    full_norm, grad_arrived, qkv_rows, qkv_cols, context, inverse, mid, arrived = front(
+        normed,
+        grad_outgoing.astype(jnp.bfloat16),
+        tokens,
+        dispatch_rows,
+        wide_qkv,
+        wide_proj,
+        score_scale,
+        local_experts,
+        1,
+    )
+    full_norm = full_norm.reshape(-1, model_width)
+    grad_arrived = grad_arrived.reshape(local_experts, -1, model_width)
+    arrived = arrived.reshape(local_experts, -1, model_width)
     normal_mid, factor_mid = norm_parts(mid)
-    mid_normed = normal_mid.astype(jnp.bfloat16)
-    outgoing = jnp.dot(dispatch_rows, mid_normed, preferred_element_type=jnp.float32).astype(
-        jnp.bfloat16
-    )
-    arrived = slots_out(outgoing, local_experts, 3).reshape(local_experts, -1, model_width)
     pre_act = jnp.einsum("end,edf->enf", arrived, up_weight, preferred_element_type=jnp.float32)
     hidden = gelu_value(pre_act).astype(jnp.bfloat16)
     expert_partial = jnp.einsum(

time: 284 us -> 260 us (0.915)
  Pallas kernels: 242 us -> 221 us
  matrix products: 28.6 us -> 21 us
  other arithmetic: 5.31 us -> 9.72 us
    pallas_call x1 -> x0, Pallas kernels: 12.1 us -> none  [attend_forward(): pl.pallas_call(partial(forward_kernel, scale), out_shape=[jax.ShapeDtypeS...]
    pallas_call x5 -> x3, Pallas kernels: 230 us -> 221 us  [comm_call(): pl.pallas_call(kernel, out_shape=out_shape, in_specs=[VM] * len(operands)...]
    dot_general x2 -> x0, matrix products: 5.93 us -> none  [the longest x1 4.96 us: shards(): jnp.einsum('ks,kd->sd', context, wide_proj, preferred_element_type=jnp.fl...]
where the time goes in v3:
time: 260 us; the launch traced here: 259 us
  Pallas kernels  221 us (85%)
  matrix products  21 us (8%)
  other arithmetic  9.72 us (4%)
  local copies, waits for them, and re-layouts  6.21 us (2%)
    pallas_call x3, Pallas kernels, comm_call(): pl.pallas_call(kernel, out_shape=out_shape, in_specs=[VM] * len(operands)...  221 us

profile of v3, /device:TPU:2, one launch (start us, length us, event | category | flops | bytes accessed | tf_op | source)
XLA Modules:
  0.0 259.2 jit_solution(673965836686161790)
XLA Ops:
  0.7 1.3 convert_reduce_fusion.1
  1.9 1.3 fusion.16
  3.9 0.8 slice_bitcast_fusion.8
  5.3 1.9 fusion.17.own_ref
  7.2 0.7 pad.9.proj_ref
  8.2 1.0 fusion.source_ref
  9.3 1.3 copy.18.weight_ref
  10.6 118.0 %shard_map.136 = (bf16[16,128,1280]{2,1,0:T(8,128)(2,1)}, bf16[2,16,32,1280]{3,2,1,0:T(8,128)(2,1)}, bf16[2048,384]{1,0:T(8,128)(2,1)}, bf16[384,2048]{1,0:T(8,1...) custom-call(bf16[128,1280]{1,0:T(8,128)(2,1)} %fusion.17.own_ref, ...), custom_call_target="tpu_custom_call" | custom-call | tf_op jit(solution)/shard_map/pallas_call | solution.py:205
  128.6 1.1 convert_reduce_fusion
  129.7 1.2 fusion.15
  130.9 3.4 %fusion.34 = f32[2,512,320]{1,2,0:T(8,128)S(1)} fusion(bf16[2,512,1280]{2,1,0:T(8,128)(2,1)} %bitcast.48, bf16[2,1280,320]{1,2,0:T(8,128)(2,1)} %param.16), kind=kOutput, calls=%fused_computation.67 | convolution fusion | flops 838860800 | bytes 5570560 | tf_op jit(solution)/shard_map/end,edf->enf/dot_general | solution.py:980
  134.3 1.2 fusion.1
  135.6 2.2 convolution_convert_fusion.3
  137.7 2.2 convolution_convert_fusion.2
  139.9 3.1 %convolution_convert_fusion = bf16[2,512,1280]{2,1,0:T(8,128)(2,1)} fusion(bf16[2,320,1280]{2,1,0:T(8,128)(2,1)S(1)} %copy-done, f32[2,512,320]{1,2,0:T(8,128)S(1)} %fusion.34), kind=kOutput, calls=%fused_computation | convolution fusion | flops 841809920 | bytes 5570560 | tf_op jit(solution)/shard_map/enf,efd->end/dot_general | solution.py:982
  143.0 3.1 %convolution_convert_fusion.1 = bf16[2,512,1280]{2,1,0:T(8,128)(2,1)} fusion(bf16[2,512,320]{1,2,0:T(8,128)(2,1)S(1)} %fusion.1, bf16[2,1280,320]{1,2,0:T(8,128)(2,1)S(1)} %copy-done.8), kind=kOutput, calls=%fused_computation.1 | convolution fusion | flops 840171520 | bytes 4915200 | tf_op jit(solution)/shard_map/enf,edf->end/dot_general | solution.py:995
  146.2 33.6 %shard_map.137 = bf16[64,1280]{1,0:T(8,128)(2,1)} custom-call(bf16[2,16,32,1280]{3,2,1,0:T(8,128)(2,1)} %bitcast.52), custom_call_target="tpu_custom_call" | custom-call | tf_op jit(solution)/shard_map/pallas_call | solution.py:205
  179.8 1.3 fusion.33
  181.1 1.0 fusion.21.own_ref
  182.1 70.0 %shard_map.138 = (bf16[64,1280]{1,0:T(8,128)(2,1)}, f32[80,320]{1,0:T(8,128)}) custom-call(bf16[128,1280]{1,0:T(8,128)(2,1)} %fusion.21.own_ref, bf16[2,16,32,1280]{3,2,1,0:T(8,128)(2,1)} %bitcast.53, bf16[2048,1280]{1,0:T(8,128)(2,1)} %bitcast.46, bf16[128,1280]{1,0:T(8,128)(2,1)} %pad.9.proj_ref, bf16[2048,384]{1,0:T(8,128)(2,1)} %get-tuple-element.20.rows_ref, ...), custom_call_target="tpu_custom_call" | custom-call | tf_op jit(solution)/shard_map/pallas_call | solution.py:205
  252.1 1.0 slice_bitcast_fusion.1
  253.1 0.9 slice_bitcast_fusion
  255.4 1.2 fusion.30
  256.6 2.1 fusion.22
  (31 shorter events, 3.7 us)
Async XLA Ops:
  0.6 133.7 %copy-start = (bf16[2,320,1280]{2,1,0:T(8,128)(2,1)S(1)}, bf16[2,320,1280]{2,1,0:T(8,128)(2,1)}, u32[]{:S(2)}) copy-start(bf16[2,320,1280]{2,1,0:T(8,128)(2,1)} %param.17) | copy-start | bytes 4915204
  0.6 7.3 %copy-start.2 = (bf16[128,1280]{1,0:T(8,128)(2,1)S(1)}, bf16[128,1280]{1,0:T(8,128)(2,1)}, u32[]{:S(2)}) copy-start(bf16[128,1280]{1,0:T(8,128)(2,1)} %param.10) | copy-start | bytes 983044
  0.7 6.6 %copy-start.6 = (bf16[1,80,1280]{2,1,0:T(8,128)(2,1)S(1)}, bf16[1,80,1280]{2,1,0:T(8,128)(2,1)}, u32[]{:S(2)}) copy-start(bf16[1,80,1280]{2,1,0:T(8,128)(2,1)} %param.15) | copy-start | bytes 614404
  1.9 7.3 %copy-start.5 = (bf16[1280,1,240]{0,2,1:T(8,128)(2,1)S(1)}, bf16[1280,1,240]{0,2,1:T(8,128)(2,1)}, u32[]{:S(2)}) copy-start(bf16[1280,1,240]{0,2,1:T(8,128)(2,1)} %param.14) | copy-start | bytes 1843204
  130.9 3.4 %copy-start.4 = (bf16[2,16,32,1280]{3,2,1,0:T(8,128)(2,1)S(1)}, bf16[2,16,32,1280]{3,2,1,0:T(8,128)(2,1)}, u32[]{:S(2)}) copy-start(bf16[2,16,32,1280]{3,2,1,0:T(8,128)(2,1)} %get-tuple-element.17) | copy-start | bytes 7864324
  135.6 2.2 copy-start.3
  139.9 3.1 %copy-start.8 = (bf16[2,1280,320]{1,2,0:T(8,128)(2,1)S(1)}, bf16[2,1280,320]{1,2,0:T(8,128)(2,1)}, u32[]{:S(2)}) copy-start(bf16[2,1280,320]{1,2,0:T(8,128)(2,1)} %param.16) | copy-start | bytes 4915204
  146.2 33.6 %copy-start.1 = (bf16[128,1280]{1,0:T(8,128)(2,1)S(1)}, bf16[128,1280]{1,0:T(8,128)(2,1)}, u32[]{:S(2)}) copy-start(bf16[128,1280]{1,0:T(8,128)(2,1)} %get-tuple-element.16) | copy-start | bytes 983044
  146.2 33.6 %copy-start.7 = (bf16[64,128]{1,0:T(8,128)(2,1)S(1)}, bf16[64,128]{1,0:T(8,128)(2,1)}, u32[]{:S(2)}) copy-start(bf16[64,128]{1,0:T(8,128)(2,1)} %fusion.31.dispatch_ref) | copy-start | bytes 49156

commit v4 on v3

--- a/solution.py
+++ b/solution.py
@@ -200,13 +200,13 @@
 GATHER_SEMS = 5
 
 
-def comm_call(kernel, out_shape, operands, scratch, ident):
-    single = not isinstance(out_shape, list)
+def comm_call(kernel, out_shape, operands, scratch, ident, far_in=0, far_out=0):
+    far = pl.BlockSpec(memory_space=pl.ANY)
     return pl.pallas_call(
         kernel,
         out_shape=out_shape,
-        in_specs=[VM] * len(operands),
-        out_specs=VM if single else [VM] * len(out_shape),
+        in_specs=[VM] * (len(operands) - far_in) + [far] * far_in,
+        out_specs=[VM] * (len(out_shape) - far_out) + [far] * far_out,
         scratch_shapes=scratch,
         compiler_params=pltpu.CompilerParams(
             collective_id=ident, has_side_effects=True, vmem_limit_bytes=60 * 1024 * 1024
@@ -447,43 +447,6 @@
 
     def finish(self):
         self.by_x.finish()
-
-
-def back_kernel(count, parts, *refs):
-    part_refs, refs = refs[:parts], refs[parts:]
-    out_refs, refs = refs[:parts], refs[parts:]
-    each = len(refs) // parts
-    rings, backs = [], []
-    for index in range(parts):
-        mine = refs[index * each : (index + 1) * each]
-        slots, ring = mine[:OUT_SCRATCH], mine[OUT_SCRATCH:]
-        rings.append(ReduceRing(part_refs[index], slots[0], *ring, count))
-        backs.append(SlotsBack(*slots[:4], out_refs[index], slots[4:]))
-    await_peers(greet_plane() + greet_ring(count))
-    for ring in rings:
-        ring.begin()
-    for ring, back in zip(rings, backs):
-        ring.run()
-        back.begin()
-    for back in backs:
-        back.middle()
-    for back in backs:
-        back.finish()
-    for ring in rings:
-        ring.finish()
-
-
-def slots_back(part_list, ident):
-    count = lax.axis_size("tensor") // 2
-    scratch, shapes = [], []
-    for part in part_list:
-        experts, _, rows, width = part.shape
-        slots = jax.ShapeDtypeStruct((experts * rows, width), part.dtype)
-        shapes.append(slots)
-        scratch += out_scratch(slots) + reduce_scratch(experts * rows, width, part.dtype, count)
-    return comm_call(
-        partial(back_kernel, count, len(part_list)), shapes, part_list, scratch, ident
-    )
 
 
 class Exchange:
@@ -789,19 +752,49 @@
     lax.fori_loop(first, last, one, 0)
 
 
+def product(left, right):
+    return lax.dot_general(
+        left, right, (((0,), (0,)), ((), ())), preferred_element_type=jnp.float32
+    )
+
+
 def closing_kernel(
     count,
     scale,
-    own_ref,
-    part_ref,
-    norm_ref,
+    gpart_ref,
+    cotangent_ref,
+    mid_ref,
+    collect_ref,
     proj_ref,
+    context_ref,
+    inverse_ref,
+    hidden_far,
+    down_far,
+    garrived_far,
+    gpre_far,
+    arrived_far,
+    rows_far,
+    cols_far,
+    norm_far,
+    slots_ref,
+    sum_ref,
+    gdown_far,
+    gup_far,
+    hidden_ref,
+    down_ref,
+    garrived_ref,
+    gpre_ref,
+    arrived_ref,
     rows_ref,
     cols_ref,
-    context_ref,
-    inverse_ref,
-    slots_ref,
-    sum_ref,
+    norm_ref,
+    gdown_ref,
+    gup_ref,
+    load_sems,
+    save_sems,
+    part_ref,
+    back_ref,
+    own_ref,
     grad_ref,
     gcols_ref,
     gkeys,
@@ -810,30 +803,87 @@
     landing,
     *refs,
 ):
+    fars = (hidden_far, down_far, garrived_far, gpre_far, arrived_far, rows_far, cols_far, norm_far)
+    nears = (hidden_ref, down_ref, garrived_ref, gpre_ref, arrived_ref, rows_ref, cols_ref, norm_ref)
+    loads = [
+        pltpu.make_async_copy(far, near, load_sems.at[index])
+        for index, (far, near) in enumerate(zip(fars, nears))
+    ]
     ring_sems, refs = refs[:GATHER_SEMS], refs[GATHER_SEMS:]
     swap_refs, refs = refs[:3], refs[3:]
-    slots, reduce = refs[:OUT_SCRATCH], refs[OUT_SCRATCH:]
+    each = OUT_SCRATCH + REDUCE_SCRATCH
+    gslots, greduce = refs[:OUT_SCRATCH], refs[OUT_SCRATCH:each]
+    slots, reduce = refs[each : each + OUT_SCRATCH], refs[each + OUT_SCRATCH :]
     _, level, _ = ring_places()
+    grad_ring = ReduceRing(gpart_ref, gslots[0], *greduce, count)
+    grad_back = SlotsBack(*gslots[:4], back_ref, gslots[4:])
     ring = GatherRing(own_ref, grad_ref, *ring_sems, count)
     back_ring = ReduceRing(part_ref, slots[0], *reduce, count)
     back = SlotsBack(*slots[:4], slots_ref, slots[4:])
     swap = Exchange(weights_ref, landing, *swap_refs)
     total = greet_groups() + greet_ring(count)
+    for load in loads:
+        load.start()
     gkeys[...] = jnp.zeros_like(gkeys)
     gvals[...] = jnp.zeros_like(gvals)
     await_peers(total)
-
-    def block(level):
+    experts = hidden_ref.shape[0]
+
+    def to_part(expert, carry):
+        block = mm(hidden_ref[expert], down_ref[expert]).astype(part_ref.dtype)
+        part_ref[expert] = block.reshape(part_ref.shape[1:])
+        return carry
+
+    def to_down(expert, carry):
+        gdown_ref[expert] = product(hidden_ref[expert], garrived_ref[expert]).astype(
+            gdown_ref.dtype
+        )
+        return carry
+
+    def to_up(expert, carry):
+        gup_ref[expert] = product(arrived_ref[expert], gpre_ref[expert]).astype(gup_ref.dtype)
+        return carry
+
+    grad_ring.begin()
+    grad_ring.run_step(0)
+    loads[0].wait()
+    loads[1].wait()
+    lax.fori_loop(0, experts, to_part, 0)
+    grad_ring.run_step(1)
+    back_ring.begin()
+    loads[2].wait()
+    lax.fori_loop(0, experts, to_down, 0)
+    save_down = pltpu.make_async_copy(gdown_ref, gdown_far, save_sems.at[0])
+    save_down.start()
+    grad_ring.run_step(2)
+    loads[3].wait()
+    loads[4].wait()
+    lax.fori_loop(0, experts, to_up, 0)
+    save_up = pltpu.make_async_copy(gup_ref, gup_far, save_sems.at[1])
+    save_up.start()
+    grad_ring.run_step(3)
+    normal, factor = norm_parts(mid_ref[...])
+    grad_ring.close()
+    grad_back.begin()
+    back_ring.run_step(0)
+    grad_back.middle()
+    back_ring.run_step(1)
+    grad_back.finish()
+    grad_norm = mm(collect_ref[...], back_ref[...])
+    grad_mid = cotangent_ref[...].astype(jnp.float32) + norm_back(normal, factor, grad_norm)
+    own_ref[...] = grad_mid.astype(own_ref.dtype)
+
+    def block(place):
         backward_block(
-            rows_ref, cols_ref, context_ref, inverse_ref, grad_ref, proj_ref, gcols_ref, gkeys, gvals, level, scale
+            rows_ref, cols_ref, context_ref, inverse_ref, grad_ref, proj_ref, gcols_ref, gkeys, gvals, place, scale
         )
 
     reach = count // 2
     ring.begin()
+    for load in loads[5:]:
+        load.wait()
     ring.settle(0, 0)
     block(level)
-    back_ring.begin()
-
     for step in range(reach):
         ring.run(step)
         for way in range(2):
@@ -841,48 +891,63 @@
         if step < reach - 1:
 
             def one_way(way, carry, step=step):
-                away = (2 * way - 1) * (step + 1)
-                block(level_at(level, away, count))
+                block(level_at(level, (2 * way - 1) * (step + 1), count))
                 return carry
 
             lax.fori_loop(0, 2, one_way, 0)
         else:
-            back_ring.run_step(0)
+            back_ring.run_step(2)
             block(level_at(level, reach, count))
     flip_sums(gcols_ref, gkeys, gvals, scale)
-    back_ring.run_step(1)
+    back_ring.run_step(3)
     parts = norm_ref.shape[1] // (2 * LANES)
-    weight_sums(norm_ref, grad_ref, context_ref, gcols_ref, weights_ref, 0, parts // 2)
-    back_ring.run_step(2)
-    weight_sums(norm_ref, grad_ref, context_ref, gcols_ref, weights_ref, parts // 2, parts)
-    swap.start()
-    back_ring.run_step(3)
+    weight_sums(norm_ref, grad_ref, context_ref, gcols_ref, weights_ref, 0, parts)
     back_ring.close()
     back.begin()
+    swap.start()
     back.middle()
+    back.finish()
     swap.finish()
     sums = landing[0].astype(jnp.float32)
     for group in range(1, landing.shape[0]):
         sums = sums + landing[group].astype(jnp.float32)
     sum_ref[...] = sums
-    back.finish()
+    save_down.wait()
+    save_up.wait()
     ring.finish()
+    grad_ring.finish()
     back_ring.finish()
 
 
-def closing(own, part, norm, proj, rows, cols, context, inverse, scale, size, ident):
+def closing(near, far, scale, size, ident):
     spots = lax.axis_size("tensor")
     count = spots // 2
     groups = lax.axis_size("dp")
-    seq, width = norm.shape
-    experts, _, slot_rows, _ = part.shape
-    slots = jax.ShapeDtypeStruct((experts * slot_rows, width), part.dtype)
+    gpart, cotangent = near[:2]
+    hidden, down, _, _, arrived = far[:5]
+    seq, width = far[-1].shape
+    experts, _, slot_rows, _ = gpart.shape
+    slots = jax.ShapeDtypeStruct((experts * slot_rows, width), gpart.dtype)
+    up_shape = (experts, width, down.shape[1])
     return comm_call(
         partial(closing_kernel, count, scale),
-        [slots, jax.ShapeDtypeStruct((width // groups, 4 * size), jnp.float32)],
-        [own, part, norm, proj, rows, cols, context, inverse],
         [
-            pltpu.VMEM((spots,) + own.shape, own.dtype),
+            slots,
+            jax.ShapeDtypeStruct((width // groups, 4 * size), jnp.float32),
+            jax.ShapeDtypeStruct(down.shape, jnp.bfloat16),
+            jax.ShapeDtypeStruct(up_shape, jnp.bfloat16),
+        ],
+        near + far,
+        [pltpu.VMEM(item.shape, item.dtype) for item in far]
+        + [
+            pltpu.VMEM(down.shape, jnp.bfloat16),
+            pltpu.VMEM(up_shape, jnp.bfloat16),
+            DMA((len(far),)),
+            DMA((2,)),
+            pltpu.VMEM(gpart.shape, gpart.dtype),
+            pltpu.VMEM(slots.shape, slots.dtype),
+            pltpu.VMEM(cotangent.shape, jnp.bfloat16),
+            pltpu.VMEM((spots,) + cotangent.shape, jnp.bfloat16),
             pltpu.VMEM((3 * size, seq), jnp.bfloat16),
             pltpu.VMEM((seq, LANES), jnp.float32),
             pltpu.VMEM((seq, LANES), jnp.float32),
@@ -891,9 +956,10 @@
         ]
         + gather_sems(count)
         + exchange_sems(groups)
-        + out_scratch(slots)
-        + reduce_scratch(experts * slot_rows, width, part.dtype, count),
+        + (out_scratch(slots) + reduce_scratch(experts * slot_rows, width, gpart.dtype, count)) * 2,
         ident,
+        len(far),
+        2,
     )
 
 
@@ -944,7 +1010,7 @@
     spots = lax.axis_size("tensor")
     local_experts = up_weight.shape[0]
     places = group_count * local_experts * CAP
-    normal_in, factor_in = norm_parts(tokens)
+    normal_in, _ = norm_parts(tokens)
     normed = normal_in.astype(jnp.bfloat16)
     slot_code = jnp.where(slot_index >= 0, routes * CAP + slot_index, -1)
     positions = jnp.arange(places, dtype=jnp.int32)
@@ -976,43 +1042,26 @@
     full_norm = full_norm.reshape(-1, model_width)
     grad_arrived = grad_arrived.reshape(local_experts, -1, model_width)
     arrived = arrived.reshape(local_experts, -1, model_width)
-    normal_mid, factor_mid = norm_parts(mid)
     pre_act = jnp.einsum("end,edf->enf", arrived, up_weight, preferred_element_type=jnp.float32)
     hidden = gelu_value(pre_act).astype(jnp.bfloat16)
-    expert_partial = jnp.einsum(
-        "enf,efd->end", hidden, down_weight, preferred_element_type=jnp.float32
-    )
     grad_hidden = jnp.einsum(
         "end,efd->enf", grad_arrived, down_weight, preferred_element_type=jnp.float32
     )
     grad_pre = (grad_hidden * gelu_slope(pre_act)).astype(jnp.bfloat16)
-    grad_down = jnp.einsum(
-        "enf,end->efd", hidden, grad_arrived, preferred_element_type=jnp.float32
-    ).astype(jnp.bfloat16)
-    grad_up = jnp.einsum(
-        "end,enf->edf", arrived, grad_pre, preferred_element_type=jnp.float32
-    ).astype(jnp.bfloat16)
     grad_partial = jnp.einsum(
         "enf,edf->end", grad_pre, up_weight, preferred_element_type=jnp.float32
     )
-    grad_partial, expert_partial = (
-        part.astype(jnp.bfloat16).reshape(local_experts, spots, -1, model_width)
-        for part in (grad_partial, expert_partial)
-    )
-    (grad_back,) = slots_back([grad_partial], 5)
-    grad_norm = jnp.einsum(
-        "pr,pd->rd", dispatch_rows, grad_back, preferred_element_type=jnp.float32
-    )
-    grad_mid = (upstream + norm_back(normal_mid, factor_mid, grad_norm)).astype(jnp.bfloat16)
-    returned, grad_weights = closing(
-        grad_mid,
-        expert_partial,
-        full_norm,
-        wide_proj,
-        qkv_rows,
-        qkv_cols,
-        context,
-        inverse,
+    returned, grad_weights, grad_down, grad_up = closing(
+        [
+            grad_partial.astype(jnp.bfloat16).reshape(local_experts, spots, -1, model_width),
+            cotangent,
+            mid,
+            dispatch_rows.T,
+            wide_proj,
+            context,
+            inverse,
+        ],
+        [hidden, down_weight, grad_arrived, grad_pre, arrived, qkv_rows, qkv_cols, full_norm],
         score_scale,
         head_size,
         6,

time: 260 us -> 245 us (0.942)
  matrix products: 21 us -> 11.6 us
  Pallas kernels: 221 us -> 216 us
  local copies, waits for them, and re-layouts: 6.21 us -> 10.3 us
  other arithmetic: 9.72 us -> 6.44 us
    dot_general x4 -> x0, matrix products: 8.74 us -> none  [the longest x1 3.09 us: shards(): jnp.einsum('enf,efd->end', hidden, down_weight, preferred_element_type=jn...]
    pallas_call x3 -> x2, Pallas kernels: 221 us -> 216 us  [comm_call(): pl.pallas_call(kernel, out_shape=out_shape, in_specs=[VM] * (len(operands...]
    unnamed x20 -> x28, local copies, waits for them, and re-layouts: 1.46 us -> 6.6 us
where the time goes in v4:
time: 245 us
  Pallas kernels  216 us (88%)
  matrix products  11.6 us (5%)
  local copies, waits for them, and re-layouts  10.3 us (4%)
  other arithmetic  6.44 us (3%)
    pallas_call x2, Pallas kernels, comm_call(): pl.pallas_call(kernel, out_shape=out_shape, in_specs=[VM] * (len(operands...  216 us
    unnamed x28, local copies, waits for them, and re-layouts  6.6 us

profile of v4, /device:TPU:2, one launch (start us, length us, event | category | flops | bytes accessed | tf_op | source)
XLA Modules:
  0.0 244.8 jit_solution(13432747152226442530)
XLA Ops:
  0.7 1.3 convert_reduce_fusion
  1.9 1.2 fusion.9
  3.2 0.8 compare_select_fusion
  3.9 0.8 slice_bitcast_fusion.8
  4.7 0.1 fusion.24
  4.8 0.6 fusion.22
  5.4 0.7 copy.39.dispatch_ref
  6.1 1.9 fusion.10.own_ref
  8.0 0.7 pad.9.proj_ref
  8.8 0.3 fusion.16
  9.0 1.0 fusion.source_ref
  10.1 1.3 copy.40.weight_ref
  11.4 117.9 %shard_map.136 = (bf16[16,128,1280]{2,1,0:T(8,128)(2,1)}, bf16[2,16,32,1280]{3,2,1,0:T(8,128)(2,1)}, bf16[2048,384]{1,0:T(8,128)(2,1)}, bf16[384,2048]{1,0:T(8,1...) custom-call(bf16[128,1280]{1,0:T(8,128)(2,1)} %fusion.10.own_ref, ...), custom_call_target="tpu_custom_call" | custom-call | tf_op jit(solution)/shard_map/pallas_call | solution.py:205
  129.4 4.3 %multiply_convert_fusion = (bf16[2,512,320]{2,1,0:T(8,128)(2,1)}, f32[2,512,320]{2,1,0:T(8,128)S(1)}) fusion(bf16[2,512,1280]{2,1,0:T(8,128)(2,1)} %bitcast.47, bf16[2,1280,320]{1,2,0:T(8,128)(2,1)S(1)} %copy-done), kind=kOutput, calls=%fused_computation.10 | convolution fusion | flops 840499200 | bytes 6225920 | tf_op jit(solution)/shard_map/end,edf->enf/dot_general | solution.py:1045
  133.7 1.6 fusion.6.gpre_far
  135.3 3.1 %convolution_convert_fusion = bf16[2,512,1280]{2,1,0:T(8,128)(2,1)} fusion(bf16[2,512,320]{2,1,0:T(8,128)(2,1)S(1)} %fusion.6.gpre_far, bf16[2,1280,320]{1,2,0:T(8,128)(2,1)S(1)} %copy-done), kind=kOutput, calls=%fused_computation | convolution fusion | flops 840171520 | bytes 4915200 | tf_op jit(solution)/shard_map/enf,edf->end/dot_general | solution.py:1051
  138.4 97.8 %shard_map.137 = (bf16[64,1280]{1,0:T(8,128)(2,1)}, f32[80,320]{1,0:T(8,128)}, bf16[2,320,1280]{2,1,0:T(8,128)(2,1)}, bf16[2,1280,320]{2,1,0:T(8,128)(2,1)}) custom-call(bf16[2,16,32,1280]{3,2,1,0:T(8,128)(2,1)} %bitcast.42, bf16[128,1280]{1,0:T(8,128)(2,1)} %cotangent_ref.1, bf16[128,1280]{1,0:T(8,128)(2,1)} %get-tuple-element.18.mid_ref, ...), custom_call_target="tpu_custom_call" | custom-call | tf_op jit(solution)/shard_map/pallas_call | solution.py:205
  236.2 3.9 %copy.51 = bf16[2,1280,320]{1,2,0:T(8,128)(2,1)} copy(bf16[2,1280,320]{2,1,0:T(8,128)(2,1)} %get-tuple-element.46) | data formatting | bytes 3276800
  240.3 0.7 copy.49
  241.0 0.7 copy.50
  241.7 0.2 fusion.21
  241.9 1.1 fusion.13
  243.0 0.6 pad_maximum_fusion
  243.6 1.2 copy.57
  (29 shorter events, 0.2 us)
Async XLA Ops:
  0.6 128.7 %copy-start = (bf16[2,1280,320]{1,2,0:T(8,128)(2,1)S(1)}, bf16[2,1280,320]{1,2,0:T(8,128)(2,1)}, u32[]{:S(2)}) copy-start(bf16[2,1280,320]{1,2,0:T(8,128)(2,1)} %param.16) | copy-start | bytes 4915204
  0.6 8.1 %copy-start.1 = (bf16[128,1280]{1,0:T(8,128)(2,1)S(1)}, bf16[128,1280]{1,0:T(8,128)(2,1)}, u32[]{:S(2)}) copy-start(bf16[128,1280]{1,0:T(8,128)(2,1)} %cotangent_ref.1) | copy-start | bytes 983044
  0.7 7.4 %copy-start.10 = (bf16[1,80,1280]{2,1,0:T(8,128)(2,1)S(1)}, bf16[1,80,1280]{2,1,0:T(8,128)(2,1)}, u32[]{:S(2)}) copy-start(bf16[1,80,1280]{2,1,0:T(8,128)(2,1)} %param.15) | copy-start | bytes 614404
  3.1 6.9 %copy-start.9 = (bf16[1280,1,240]{0,2,1:T(8,128)(2,1)S(1)}, bf16[1280,1,240]{0,2,1:T(8,128)(2,1)}, u32[]{:S(2)}) copy-start(bf16[1280,1,240]{0,2,1:T(8,128)(2,1)} %param.14) | copy-start | bytes 1843204
  129.3 4.3 %copy-start.4 = (bf16[2,16,32,1280]{3,2,1,0:T(8,128)(2,1)S(1)}, bf16[2,16,32,1280]{3,2,1,0:T(8,128)(2,1)}, u32[]{:S(2)}) copy-start(bf16[2,16,32,1280]{3,2,1,0:T(8,128)(2,1)} %get-tuple-element.19) | copy-start | bytes 7864324
  129.3 4.3 %copy-start.5 = (bf16[2,320,1280]{2,1,0:T(8,128)(2,1)S(1)}, bf16[2,320,1280]{2,1,0:T(8,128)(2,1)}, u32[]{:S(2)}) copy-start(bf16[2,320,1280]{2,1,0:T(8,128)(2,1)} %down_far.1) | copy-start | bytes 4915204
  135.3 3.1 %copy-start.3 = (bf16[2,512,320]{2,1,0:T(8,128)(2,1)}, bf16[2,512,320]{2,1,0:T(8,128)(2,1)S(1)}, u32[]{:S(2)}) copy-start(bf16[2,512,320]{2,1,0:T(8,128)(2,1)S(1)} %fusion.6.gpre_far) | copy-start | bytes 1966084
  236.2 4.0 %copy-start.11 = (f32[80,320]{1,0:T(8,128)S(1)}, f32[80,320]{1,0:T(8,128)}, u32[]{:S(2)}) copy-start(f32[80,320]{1,0:T(8,128)} %get-tuple-element.27) | copy-start | bytes 307204
  236.2 5.5 %copy-start.8 = (bf16[64,1280]{1,0:T(8,128)(2,1)S(1)}, bf16[64,1280]{1,0:T(8,128)(2,1)}, u32[]{:S(2)}) copy-start(bf16[64,1280]{1,0:T(8,128)(2,1)} %get-tuple-element.26) | copy-start | bytes 491524
  236.2 5.7 %copy-start.2 = (bf16[128,1280]{1,0:T(8,128)(2,1)S(1)}, bf16[128,1280]{1,0:T(8,128)(2,1)}, u32[]{:S(2)}) copy-start(bf16[128,1280]{1,0:T(8,128)(2,1)} %cotangent_ref.1) | copy-start | bytes 983044
  236.2 5.7 %copy-start.7 = (bf16[128,1280]{1,0:T(8,128)(2,1)S(1)}, bf16[128,1280]{1,0:T(8,128)(2,1)}, u32[]{:S(2)}) copy-start(bf16[128,1280]{1,0:T(8,128)(2,1)} %get-tuple-element.18.mid_ref) | copy-start | bytes 983044
  241.7 1.9 copy-start.6

commit v5 on v4

--- a/solution.py
+++ b/solution.py
@@ -64,12 +64,12 @@
     return 2 * (SIDE - 1)
 
 
-def greet_groups():
-    me = lax.axis_index("dp")
-    count = lax.axis_size("dp")
+def greet_axis(axis):
+    me = lax.axis_index(axis)
+    count = lax.axis_size(axis)
 
     def call(step, carry):
-        signal("dp", lax.rem(me + step, count))
+        signal(axis, lax.rem(me + step, count))
         return carry
 
     lax.fori_loop(1, count, call, 0)
@@ -517,9 +517,7 @@
     cols_ref[:, rows] = block.T.astype(cols_ref.dtype)
 
 
-def attend_block(
-    rows_ref, cols_ref, context_ref, inverse_ref, raised_ref, context_rows, index, scale
-):
+def attend_block(rows_ref, cols_ref, context_ref, inverse_ref, raised_ref, index, scale):
     seq = rows_ref.shape[0]
     here = pl.ds(pl.multiple_of(index * QUERY_BLOCK, QUERY_BLOCK), QUERY_BLOCK)
     queries = cols_ref[0:LANES, here]
@@ -536,7 +534,193 @@
         shares = (raised_ref[at : at + KEY_BLOCK, :] * inverse).astype(jnp.bfloat16)
         context = context + mm(cols_ref[2 * LANES : 3 * LANES, at : at + KEY_BLOCK], shares)
     context_ref[:, here] = context.astype(context_ref.dtype)
-    context_rows[here, :] = context.T.astype(context_rows.dtype)
+
+
+def product(left, right):
+    return lax.dot_general(
+        left, right, (((0,), (0,)), ((), ())), preferred_element_type=jnp.float32
+    )
+
+
+class HeadWeights:
+    def __init__(self, own_ref, half_ref, full_ref, count, sems):
+        self.spot, self.level, self.side = ring_places()
+        self.peers = ring_peers(count)
+        self.me = lax.axis_index("dp")
+        self.groups = lax.axis_size("dp")
+        self.count = count
+        self.away = level_at(self.level, count - lax.div(self.me, 2), count)
+        self.at_home = self.spot == self.me
+        self.own, self.half, self.full = own_ref, half_ref, full_ref
+        self.chain_send, self.chain_recv, self.chain_keep = sems[:3]
+        self.send, self.recv, self.keep_sem, self.give, self.take = sems[3:]
+
+    def lanes(self, side):
+        width = self.half.shape[1]
+        return pl.ds(pl.multiple_of(side * width, LANES), width)
+
+    def to_partner(self):
+        source = self.own.at[:, self.lanes(1 - self.side)]
+        return remote(
+            source, self.half, self.chain_send.at[2], self.chain_recv, "tensor", self.peers[2]
+        )
+
+    def onward(self, way):
+        return remote(
+            self.half, self.half, self.chain_send.at[way], self.chain_recv, "tensor", self.peers[way]
+        )
+
+    def begin(self):
+        @pl.when(self.at_home)
+        def _():
+            self.to_partner().start()
+            keep = pltpu.make_async_copy(
+                self.own.at[:, self.lanes(self.side)], self.half, self.chain_keep
+            )
+            keep.start()
+            keep.wait()
+            self.onward(0).start()
+            self.onward(1).start()
+            self.spread()
+
+    def pass_on(self, distance):
+        if distance == 0:
+
+            @pl.when(jnp.logical_and(self.away == 0, jnp.logical_not(self.at_home)))
+            def _():
+                self.onward(0).wait_recv()
+                self.onward(0).start()
+                self.onward(1).start()
+                self.spread()
+
+            return
+        reach = self.count // 2
+
+        @pl.when(self.away == distance)
+        def _():
+            self.onward(0).wait_recv()
+            if distance < reach:
+                self.onward(0).start()
+            self.spread()
+
+        if distance < reach:
+
+            @pl.when(self.away == self.count - distance)
+            def _():
+                self.onward(1).wait_recv()
+                if distance < reach - 1:
+                    self.onward(1).start()
+                self.spread()
+
+    def put(self, step):
+        peer = lax.rem(self.me + step, self.groups)
+        target = self.full.at[self.me, :, self.lanes(self.side)]
+        return remote(self.half, target, self.send.at[step], self.recv.at[step], "dp", peer)
+
+    def keep(self):
+        target = self.full.at[self.me, :, self.lanes(self.side)]
+        return pltpu.make_async_copy(self.half, target, self.keep_sem)
+
+    def spread(self):
+        def put_one(step, carry):
+            self.put(step).start()
+            return carry
+
+        lax.fori_loop(1, self.groups, put_one, 0)
+        self.keep().start()
+
+    def across(self, step, side):
+        head = lax.rem(self.me - step + self.groups, self.groups)
+        block = self.full.at[head, :, self.lanes(side)]
+        return remote(
+            block, block, self.give.at[step], self.take.at[step], "tensor", self.peers[2]
+        )
+
+    def swap_halves(self):
+        self.keep().wait()
+        self.across(0, self.side).start()
+
+        def one(step, carry):
+            head = lax.rem(self.me - step + self.groups, self.groups)
+            block = self.full.at[head, :, self.lanes(self.side)]
+            remote(
+                self.half, block, self.send.at[step], self.recv.at[step], "dp", head
+            ).wait_recv()
+            self.across(step, self.side).start()
+            return carry
+
+        lax.fori_loop(1, self.groups, one, 0)
+
+    def settle(self):
+        def one(step, carry):
+            self.across(step, 1 - self.side).wait_recv()
+            return carry
+
+        lax.fori_loop(0, self.groups, one, 0)
+
+    def finish(self):
+        reach = self.count // 2
+
+        @pl.when(self.at_home)
+        def _():
+            self.to_partner().wait_send()
+
+        @pl.when(self.away < reach)
+        def _():
+            self.onward(0).wait_send()
+
+        @pl.when(jnp.logical_or(self.away == 0, self.away > reach + 1))
+        def _():
+            self.onward(1).wait_send()
+
+        def one(step, carry):
+            self.put(step).wait_send()
+            return carry
+
+        lax.fori_loop(1, self.groups, one, 0)
+
+        def two(step, carry):
+            self.across(step, self.side).wait_send()
+            return carry
+
+        lax.fori_loop(0, self.groups, two, 0)
+
+
+class ContextSwap:
+    def __init__(self, context_ref, target_ref, send, recv, mine):
+        self.spot = lax.axis_index("tensor")
+        self.count = lax.axis_size("tensor")
+        self.refs = (context_ref, target_ref, send, recv)
+        self.keep = pltpu.make_async_copy(self.block(self.spot), target_ref.at[self.spot], mine)
+
+    def block(self, spot):
+        context_ref, target_ref = self.refs[:2]
+        _, size, rows = target_ref.shape
+        return context_ref.at[pl.ds(0, size), pl.ds(pl.multiple_of(spot * rows, rows), rows)]
+
+    def copy(self, step, outward):
+        _, target_ref, send, recv = self.refs
+        peer = lax.rem(self.spot + (step if outward else self.count - step), self.count)
+        target = target_ref.at[self.spot if outward else peer]
+        return remote(self.block(peer), target, send.at[step], recv.at[step], "tensor", peer)
+
+    def start(self):
+        def one(step, carry):
+            self.copy(step, True).start()
+            return carry
+
+        lax.fori_loop(1, self.count, one, 0)
+        self.keep.start()
+
+    def finish(self):
+        self.keep.wait()
+
+        def one(step, carry):
+            self.copy(step, False).wait_recv()
+            self.copy(step, True).wait_send()
+            return carry
+
+        lax.fori_loop(1, self.count, one, 0)
 
 
 def front_kernel(
@@ -557,9 +741,9 @@
     mid_ref,
     arrived_ref,
     raised_ref,
-    context_rows,
-    part_ref,
-    total_ref,
+    half_ref,
+    heads_ref,
+    context_all,
     outgoing_ref,
     *refs,
 ):
@@ -568,13 +752,14 @@
     grads, refs = refs[:OUT_SCRATCH], refs[OUT_SCRATCH:]
     slots, refs = refs[:OUT_SCRATCH], refs[OUT_SCRATCH:]
     sems, refs = refs[: 3 * GATHER_SEMS], refs[3 * GATHER_SEMS :]
+    weights = HeadWeights(proj_ref, half_ref, heads_ref, count, refs[:8])
+    contexts = ContextSwap(context_ref, context_all, *refs[8:])
     grads_out = SlotsOut(source_ref, *grads[:4], grads[4:])
     slots_out = SlotsOut(outgoing_ref, *slots[:4], slots[4:])
     first = GatherRing(own_ref, norm_ref, *sems[:GATHER_SEMS], count)
     second = GatherRing(grads[3], gslots_ref, *sems[GATHER_SEMS : 2 * GATHER_SEMS], count)
     third = GatherRing(slots[3], arrived_ref, *sems[2 * GATHER_SEMS :], count)
-    reduce = ReduceRing(part_ref, total_ref, *refs, count)
-    await_peers(greet_plane() + greet_ring(count))
+    await_peers(greet_axis("dp") + greet_axis("tensor"))
 
     def both_ways(act, distance):
         def one_way(way, carry):
@@ -588,22 +773,19 @@
 
     def attend(index, carry):
         attend_block(
-            rows_ref, cols_ref, context_ref, inverse_ref, raised_ref, context_rows, index, scale
+            rows_ref, cols_ref, context_ref, inverse_ref, raised_ref, index, scale
         )
         return carry
-
-    def fill_part(place):
-        size = 2 * part_ref.shape[1]
-        rows = pl.ds(pl.multiple_of(place * size, size), size)
-        block = mm(context_rows[rows, :], proj_ref[...]).astype(part_ref.dtype)
-        part_ref[pl.ds(place * 2, 2)] = block.reshape(2, part_ref.shape[1], part_ref.shape[2])
 
     grads_out.begin()
     first.begin()
+    weights.begin()
     first.settle(0, 0)
     project(level)
+    weights.pass_on(0)
     for step in range(reach):
         first.run(step)
+        weights.pass_on(step + 1)
         if step == 0:
             grads_out.middle()
         if step == 1:
@@ -621,26 +803,20 @@
     second.run(0)
     second.run(1)
     lax.fori_loop(blocks // 2, blocks, attend, 0)
+    contexts.start()
     second.run(2)
-    fill_part(level_at(level, reach, count))
-    reduce.begin_step(0)
-    both_ways(fill_part, reach - 1)
-    reduce.begin_step(1)
+    weights.swap_halves()
     second.run(3)
-    reduce.run_step(0)
-    both_ways(fill_part, reach - 2)
-    reduce.begin_step(2)
-    reduce.run_step(1)
-    both_ways(fill_part, reach - 3)
-    reduce.begin_step(3)
-    fill_part(level)
-    reduce.begin_step(reach)
-    reduce.run_step(2)
-    reduce.run_step(3)
     first.finish()
     second.finish()
-    reduce.close()
-    mid = (tokens_ref[...].astype(jnp.float32) + total_ref[...]).astype(mid_ref.dtype)
+    contexts.finish()
+    weights.settle()
+    spots, size, rows = context_all.shape
+    attention = product(
+        context_all[...].reshape(spots * size, rows),
+        heads_ref[...].reshape(spots * size, heads_ref.shape[2]),
+    )
+    mid = (tokens_ref[...].astype(jnp.float32) + attention).astype(mid_ref.dtype)
     mid_ref[...] = mid
     normal, _ = norm_parts(mid)
     outgoing_ref[...] = mm(dispatch_ref[...], normal.astype(jnp.bfloat16)).astype(
@@ -653,7 +829,7 @@
     for step in range(reach):
         third.run(step)
     third.finish()
-    reduce.finish()
+    weights.finish()
 
 
 def front(own, grad_slots, tokens, dispatch, weight, proj, scale, local_experts, ident):
@@ -661,6 +837,7 @@
     count = spots // 2
     rows, width = own.shape
     seq = spots * rows
+    size = proj.shape[0]
     return comm_call(
         partial(front_kernel, count, scale),
         [
@@ -676,15 +853,17 @@
         [own, grad_slots, tokens, dispatch, weight, proj],
         [
             pltpu.VMEM((seq, QUERY_BLOCK), jnp.float32),
-            pltpu.VMEM((seq, LANES), jnp.bfloat16),
-            pltpu.VMEM((spots, rows, width), jnp.bfloat16),
-            pltpu.VMEM((rows, width), jnp.float32),
+            pltpu.VMEM((size, width // 2), jnp.bfloat16),
+            pltpu.VMEM((spots, size, width), jnp.bfloat16),
+            pltpu.VMEM((spots, size, rows), jnp.bfloat16),
             pltpu.VMEM(grad_slots.shape, grad_slots.dtype),
         ]
         + out_scratch(grad_slots)
         + out_scratch(grad_slots)
         + gather_sems(count) * 3
-        + reduce_scratch(rows, width, jnp.bfloat16, count),
+        + [DMA((3,)), DMA(()), DMA(())]
+        + [DMA((spots,)), DMA((spots,)), DMA(()), DMA((spots,)), DMA((spots,))]
+        + [DMA((spots,)), DMA((spots,)), DMA(())],
         ident,
     )
 
@@ -750,12 +929,6 @@
         return carry
 
     lax.fori_loop(first, last, one, 0)
-
-
-def product(left, right):
-    return lax.dot_general(
-        left, right, (((0,), (0,)), ((), ())), preferred_element_type=jnp.float32
-    )
 
 
 def closing_kernel(
@@ -821,7 +994,7 @@
     back_ring = ReduceRing(part_ref, slots[0], *reduce, count)
     back = SlotsBack(*slots[:4], slots_ref, slots[4:])
     swap = Exchange(weights_ref, landing, *swap_refs)
-    total = greet_groups() + greet_ring(count)
+    total = greet_axis("dp") + greet_ring(count)
     for load in loads:
         load.start()
     gkeys[...] = jnp.zeros_like(gkeys)
@@ -841,7 +1014,7 @@
         return carry
 
     def to_up(expert, carry):
-        gup_ref[expert] = product(arrived_ref[expert], gpre_ref[expert]).astype(gup_ref.dtype)
+        gup_ref[expert] = product(gpre_ref[expert], arrived_ref[expert]).astype(gup_ref.dtype)
         return carry
 
     grad_ring.begin()
@@ -928,20 +1101,19 @@
     seq, width = far[-1].shape
     experts, _, slot_rows, _ = gpart.shape
     slots = jax.ShapeDtypeStruct((experts * slot_rows, width), gpart.dtype)
-    up_shape = (experts, width, down.shape[1])
     return comm_call(
         partial(closing_kernel, count, scale),
         [
             slots,
             jax.ShapeDtypeStruct((width // groups, 4 * size), jnp.float32),
             jax.ShapeDtypeStruct(down.shape, jnp.bfloat16),
-            jax.ShapeDtypeStruct(up_shape, jnp.bfloat16),
+            jax.ShapeDtypeStruct(down.shape, jnp.bfloat16),
         ],
         near + far,
         [pltpu.VMEM(item.shape, item.dtype) for item in far]
         + [
             pltpu.VMEM(down.shape, jnp.bfloat16),
-            pltpu.VMEM(up_shape, jnp.bfloat16),
+            pltpu.VMEM(down.shape, jnp.bfloat16),
             DMA((len(far),)),
             DMA((2,)),
             pltpu.VMEM(gpart.shape, gpart.dtype),
@@ -1034,7 +1206,7 @@
         tokens,
         dispatch_rows,
         wide_qkv,
-        wide_proj,
+        proj_weight[0],
         score_scale,
         local_experts,
         1,
@@ -1078,7 +1250,7 @@
     )
     grad_qkv = grad_weights[:, None, : 3 * head_size]
     grad_proj = grad_weights[:, 3 * head_size :].T[None]
-    return (layer_out, gate_grad, grad_qkv, grad_proj, grad_up, grad_down)
+    return (layer_out, gate_grad, grad_qkv, grad_proj, grad_up.swapaxes(1, 2), grad_down)
 
 
 def solution(mesh):

time: 245 us -> 231 us (0.943)
  Pallas kernels: 216 us -> 200 us
    pallas_call x2, Pallas kernels: 216 us -> 200 us  [comm_call(): pl.pallas_call(kernel, out_shape=out_shape, in_specs=[VM] * (len(operands...]
    unnamed x28 -> x26, local copies, waits for them, and re-layouts: 6.6 us -> 4.66 us
where the time goes in v5:
time: 231 us
  Pallas kernels  200 us (87%)
  matrix products  13.5 us (6%)
  local copies, waits for them, and re-layouts  10.1 us (4%)
  other arithmetic  6.43 us (3%)
    pallas_call x2, Pallas kernels, comm_call(): pl.pallas_call(kernel, out_shape=out_shape, in_specs=[VM] * (len(operands...  200 us
    unnamed x26, local copies, waits for them, and re-layouts  4.66 us

profile of v5, /device:TPU:2, one launch (start us, length us, event | category | flops | bytes accessed | tf_op | source)
XLA Modules:
  0.0 230.7 jit_solution(15650481367295694761)
XLA Ops:
  0.7 1.2 convert_reduce_fusion
  1.9 1.2 fusion.9
  3.2 0.8 compare_select_fusion
  3.9 0.8 slice_bitcast_fusion.8
  4.8 0.6 fusion.22
  5.4 0.7 copy.37.dispatch_ref
  6.1 1.9 fusion.10.own_ref
  8.3 1.0 fusion.source_ref
  9.2 0.7 pad.9.proj_ref
  10.1 1.3 copy.38.weight_ref
  11.4 102.4 %shard_map.136 = (bf16[16,128,1280]{2,1,0:T(8,128)(2,1)}, bf16[2,16,32,1280]{3,2,1,0:T(8,128)(2,1)}, bf16[2048,384]{1,0:T(8,128)(2,1)}, bf16[384,2048]{1,0:T(8,1...) custom-call(bf16[128,1280]{1,0:T(8,128)(2,1)} %fusion.10.own_ref, ...), custom_call_target="tpu_custom_call" | custom-call | tf_op jit(solution)/shard_map/pallas_call | solution.py:205
  113.8 4.3 %multiply_convert_fusion = (bf16[2,512,320]{2,1,0:T(8,128)(2,1)}, f32[2,512,320]{2,1,0:T(8,128)S(1)}) fusion(bf16[2,512,1280]{2,1,0:T(8,128)(2,1)} %bitcast.48, bf16[2,1280,320]{1,2,0:T(8,128)(2,1)S(1)} %copy-done), kind=kOutput, calls=%fused_computation.10 | convolution fusion | flops 840499200 | bytes 6225920 | tf_op jit(solution)/shard_map/end,edf->enf/dot_general | solution.py:1217
  118.1 1.6 fusion.6.gpre_far
  119.8 3.1 %convolution_convert_fusion = bf16[2,512,1280]{2,1,0:T(8,128)(2,1)} fusion(bf16[2,512,320]{2,1,0:T(8,128)(2,1)S(1)} %fusion.6.gpre_far, bf16[2,1280,320]{1,2,0:T(8,128)(2,1)S(1)} %copy-done), kind=kOutput, calls=%fused_computation | convolution fusion | flops 840171520 | bytes 4915200 | tf_op jit(solution)/shard_map/enf,edf->end/dot_general | solution.py:1223
  122.9 97.5 %shard_map.137 = (bf16[64,1280]{1,0:T(8,128)(2,1)}, f32[80,320]{1,0:T(8,128)}, bf16[2,320,1280]{2,1,0:T(8,128)(2,1)}, bf16[2,320,1280]{2,1,0:T(8,128)(2,1)}) custom-call(bf16[2,16,32,1280]{3,2,1,0:T(8,128)(2,1)} %bitcast.43, bf16[128,1280]{1,0:T(8,128)(2,1)} %cotangent_ref.1, bf16[128,1280]{1,0:T(8,128)(2,1)} %get-tuple-element.18.mid_ref, ...), custom_call_target="tpu_custom_call" | custom-call | tf_op jit(solution)/shard_map/pallas_call | solution.py:205
  220.4 1.0 slice_bitcast_fusion.7
  221.4 0.9 slice_bitcast_fusion
  222.3 0.7 copy.47
  223.0 0.7 copy.48
  223.7 1.3 fusion.21
  225.0 2.0 fusion.13
  227.5 1.2 copy.55
  228.7 0.9 copy-done.6
  229.6 1.2 copy.56
  (27 shorter events, 1.1 us)
Async XLA Ops:
  0.6 113.2 %copy-start = (bf16[2,1280,320]{1,2,0:T(8,128)(2,1)S(1)}, bf16[2,1280,320]{1,2,0:T(8,128)(2,1)}, u32[]{:S(2)}) copy-start(bf16[2,1280,320]{1,2,0:T(8,128)(2,1)} %param.16) | copy-start | bytes 4915204
  0.6 7.4 %copy-start.1 = (bf16[128,1280]{1,0:T(8,128)(2,1)S(1)}, bf16[128,1280]{1,0:T(8,128)(2,1)}, u32[]{:S(2)}) copy-start(bf16[128,1280]{1,0:T(8,128)(2,1)} %cotangent_ref.1) | copy-start | bytes 983044
  0.7 8.6 %copy-start.9 = (bf16[1,80,1280]{2,1,0:T(8,128)(2,1)S(1)}, bf16[1,80,1280]{2,1,0:T(8,128)(2,1)}, u32[]{:S(2)}) copy-start(bf16[1,80,1280]{2,1,0:T(8,128)(2,1)} %param.15) | copy-start | bytes 614404
  3.1 6.9 %copy-start.10 = (bf16[1280,1,240]{0,2,1:T(8,128)(2,1)S(1)}, bf16[1280,1,240]{0,2,1:T(8,128)(2,1)}, u32[]{:S(2)}) copy-start(bf16[1280,1,240]{0,2,1:T(8,128)(2,1)} %param.14) | copy-start | bytes 1843204
  113.8 4.3 %copy-start.4 = (bf16[2,16,32,1280]{3,2,1,0:T(8,128)(2,1)S(1)}, bf16[2,16,32,1280]{3,2,1,0:T(8,128)(2,1)}, u32[]{:S(2)}) copy-start(bf16[2,16,32,1280]{3,2,1,0:T(8,128)(2,1)} %get-tuple-element.19) | copy-start | bytes 7864324
  113.8 4.3 %copy-start.5 = (bf16[2,320,1280]{2,1,0:T(8,128)(2,1)S(1)}, bf16[2,320,1280]{2,1,0:T(8,128)(2,1)}, u32[]{:S(2)}) copy-start(bf16[2,320,1280]{2,1,0:T(8,128)(2,1)} %down_far.1) | copy-start | bytes 4915204
  119.8 3.1 %copy-start.3 = (bf16[2,512,320]{2,1,0:T(8,128)(2,1)}, bf16[2,512,320]{2,1,0:T(8,128)(2,1)S(1)}, u32[]{:S(2)}) copy-start(bf16[2,512,320]{2,1,0:T(8,128)(2,1)S(1)} %fusion.6.gpre_far) | copy-start | bytes 1966084
  122.9 102.1 %copy-start.2 = (bf16[128,1280]{1,0:T(8,128)(2,1)S(1)}, bf16[128,1280]{1,0:T(8,128)(2,1)}, u32[]{:S(2)}) copy-start(bf16[128,1280]{1,0:T(8,128)(2,1)} %cotangent_ref.1) | copy-start | bytes 983044
  122.9 102.1 %copy-start.8 = (bf16[128,1280]{1,0:T(8,128)(2,1)S(1)}, bf16[128,1280]{1,0:T(8,128)(2,1)}, u32[]{:S(2)}) copy-start(bf16[128,1280]{1,0:T(8,128)(2,1)} %get-tuple-element.18.mid_ref) | copy-start | bytes 983044
  223.7 3.9 %copy-start.7 = (bf16[2,320,1280]{2,1,0:T(8,128)(2,1)S(1)}, bf16[2,320,1280]{2,1,0:T(8,128)(2,1)}, u32[]{:S(2)}) copy-start(bf16[2,320,1280]{2,1,0:T(8,128)(2,1)} %get-tuple-element.28) | copy-start | bytes 4915204
  227.5 2.0 copy-start.6

commit v6 on v5

--- a/solution.py
+++ b/solution.py
@@ -801,14 +801,10 @@
     blocks = norm_ref.shape[0] * norm_ref.shape[1] // QUERY_BLOCK
     lax.fori_loop(0, blocks // 2, attend, 0)
     second.run(0)
-    second.run(1)
     lax.fori_loop(blocks // 2, blocks, attend, 0)
     contexts.start()
-    second.run(2)
     weights.swap_halves()
-    second.run(3)
     first.finish()
-    second.finish()
     contexts.finish()
     weights.settle()
     spots, size, rows = context_all.shape
@@ -823,11 +819,15 @@
         outgoing_ref.dtype
     )
     slots_out.begin()
+    second.run(1)
     slots_out.middle()
+    second.run(2)
     slots_out.finish()
     third.begin()
+    second.run(3)
     for step in range(reach):
         third.run(step)
+    second.finish()
     third.finish()
     weights.finish()
 
@@ -1059,6 +1059,8 @@
     block(level)
     for step in range(reach):
         ring.run(step)
+        if step >= 2:
+            back_ring.run_step(step)
         for way in range(2):
             ring.settle(way, step + 1)
         if step < reach - 1:
@@ -1069,10 +1071,8 @@
 
             lax.fori_loop(0, 2, one_way, 0)
         else:
-            back_ring.run_step(2)
             block(level_at(level, reach, count))
     flip_sums(gcols_ref, gkeys, gvals, scale)
-    back_ring.run_step(3)
     parts = norm_ref.shape[1] // (2 * LANES)
     weight_sums(norm_ref, grad_ref, context_ref, gcols_ref, weights_ref, 0, parts)
     back_ring.close()

time: 231 us -> 223 us (0.965)
  Pallas kernels: 200 us -> 190 us
    pallas_call x2, Pallas kernels: 200 us -> 190 us  [comm_call(): pl.pallas_call(kernel, out_shape=out_shape, in_specs=[VM] * (len(operands...]
where the time goes in v6:
time: 223 us; the launch traced here: 221 us
  Pallas kernels  190 us (85%)
  matrix products  13.5 us (6%)
  local copies, waits for them, and re-layouts  10.1 us (5%)
  other arithmetic  6.43 us (3%)
    pallas_call x2, Pallas kernels, comm_call(): pl.pallas_call(kernel, out_shape=out_shape, in_specs=[VM] * (len(operands...  190 us
    unnamed x26, local copies, waits for them, and re-layouts  4.66 us

profile of v6, /device:TPU:2, one launch (start us, length us, event | category | flops | bytes accessed | tf_op | source)
XLA Modules:
  0.0 220.9 jit_solution(11192622231129618054)
XLA Ops:
  0.7 1.2 convert_reduce_fusion
  1.9 1.2 fusion.9
  3.2 0.8 compare_select_fusion
  3.9 0.8 slice_bitcast_fusion.8
  4.8 0.6 fusion.22
  5.4 0.7 copy.37.dispatch_ref
  6.1 1.9 fusion.10.own_ref
  8.3 1.0 fusion.source_ref
  9.2 0.7 pad.9.proj_ref
  10.1 1.3 copy.38.weight_ref
  11.4 97.2 %shard_map.136 = (bf16[16,128,1280]{2,1,0:T(8,128)(2,1)}, bf16[2,16,32,1280]{3,2,1,0:T(8,128)(2,1)}, bf16[2048,384]{1,0:T(8,128)(2,1)}, bf16[384,2048]{1,0:T(8,1...) custom-call(bf16[128,1280]{1,0:T(8,128)(2,1)} %fusion.10.own_ref, ...), custom_call_target="tpu_custom_call" | custom-call | tf_op jit(solution)/shard_map/pallas_call | solution.py:205
  108.6 4.3 %multiply_convert_fusion = (bf16[2,512,320]{2,1,0:T(8,128)(2,1)}, f32[2,512,320]{2,1,0:T(8,128)S(1)}) fusion(bf16[2,512,1280]{2,1,0:T(8,128)(2,1)} %bitcast.48, bf16[2,1280,320]{1,2,0:T(8,128)(2,1)S(1)} %copy-done), kind=kOutput, calls=%fused_computation.10 | convolution fusion | flops 840499200 | bytes 6225920 | tf_op jit(solution)/shard_map/end,edf->enf/dot_general | solution.py:1217
  112.9 1.6 fusion.6.gpre_far
  114.6 3.0 %convolution_convert_fusion = bf16[2,512,1280]{2,1,0:T(8,128)(2,1)} fusion(bf16[2,512,320]{2,1,0:T(8,128)(2,1)S(1)} %fusion.6.gpre_far, bf16[2,1280,320]{1,2,0:T(8,128)(2,1)S(1)} %copy-done), kind=kOutput, calls=%fused_computation | convolution fusion | flops 840171520 | bytes 4915200 | tf_op jit(solution)/shard_map/enf,edf->end/dot_general | solution.py:1223
  117.6 92.9 %shard_map.137 = (bf16[64,1280]{1,0:T(8,128)(2,1)}, f32[80,320]{1,0:T(8,128)}, bf16[2,320,1280]{2,1,0:T(8,128)(2,1)}, bf16[2,320,1280]{2,1,0:T(8,128)(2,1)}) custom-call(bf16[2,16,32,1280]{3,2,1,0:T(8,128)(2,1)} %bitcast.43, bf16[128,1280]{1,0:T(8,128)(2,1)} %cotangent_ref.1, bf16[128,1280]{1,0:T(8,128)(2,1)} %get-tuple-element.18.mid_ref, ...), custom_call_target="tpu_custom_call" | custom-call | tf_op jit(solution)/shard_map/pallas_call | solution.py:205
  210.5 1.0 slice_bitcast_fusion.7
  211.5 0.9 slice_bitcast_fusion
  212.4 0.7 copy.47
  213.1 0.7 copy.48
  213.8 1.3 fusion.21
  215.1 2.0 fusion.13
  217.7 1.2 copy.55
  218.8 0.9 copy-done.6
  219.7 1.2 copy.56
  (27 shorter events, 1.1 us)
Async XLA Ops:
  0.6 107.9 %copy-start = (bf16[2,1280,320]{1,2,0:T(8,128)(2,1)S(1)}, bf16[2,1280,320]{1,2,0:T(8,128)(2,1)}, u32[]{:S(2)}) copy-start(bf16[2,1280,320]{1,2,0:T(8,128)(2,1)} %param.16) | copy-start | bytes 4915204
  0.6 7.4 %copy-start.1 = (bf16[128,1280]{1,0:T(8,128)(2,1)S(1)}, bf16[128,1280]{1,0:T(8,128)(2,1)}, u32[]{:S(2)}) copy-start(bf16[128,1280]{1,0:T(8,128)(2,1)} %cotangent_ref.1) | copy-start | bytes 983044
  0.7 8.6 %copy-start.9 = (bf16[1,80,1280]{2,1,0:T(8,128)(2,1)S(1)}, bf16[1,80,1280]{2,1,0:T(8,128)(2,1)}, u32[]{:S(2)}) copy-start(bf16[1,80,1280]{2,1,0:T(8,128)(2,1)} %param.15) | copy-start | bytes 614404
  3.1 6.9 %copy-start.10 = (bf16[1280,1,240]{0,2,1:T(8,128)(2,1)S(1)}, bf16[1280,1,240]{0,2,1:T(8,128)(2,1)}, u32[]{:S(2)}) copy-start(bf16[1280,1,240]{0,2,1:T(8,128)(2,1)} %param.14) | copy-start | bytes 1843204
  108.6 4.3 %copy-start.4 = (bf16[2,16,32,1280]{3,2,1,0:T(8,128)(2,1)S(1)}, bf16[2,16,32,1280]{3,2,1,0:T(8,128)(2,1)}, u32[]{:S(2)}) copy-start(bf16[2,16,32,1280]{3,2,1,0:T(8,128)(2,1)} %get-tuple-element.19) | copy-start | bytes 7864324
  108.6 4.3 %copy-start.5 = (bf16[2,320,1280]{2,1,0:T(8,128)(2,1)S(1)}, bf16[2,320,1280]{2,1,0:T(8,128)(2,1)}, u32[]{:S(2)}) copy-start(bf16[2,320,1280]{2,1,0:T(8,128)(2,1)} %down_far.1) | copy-start | bytes 4915204
  114.5 3.1 %copy-start.3 = (bf16[2,512,320]{2,1,0:T(8,128)(2,1)}, bf16[2,512,320]{2,1,0:T(8,128)(2,1)S(1)}, u32[]{:S(2)}) copy-start(bf16[2,512,320]{2,1,0:T(8,128)(2,1)S(1)} %fusion.6.gpre_far) | copy-start | bytes 1966084
  117.6 97.5 %copy-start.2 = (bf16[128,1280]{1,0:T(8,128)(2,1)S(1)}, bf16[128,1280]{1,0:T(8,128)(2,1)}, u32[]{:S(2)}) copy-start(bf16[128,1280]{1,0:T(8,128)(2,1)} %cotangent_ref.1) | copy-start | bytes 983044
  117.6 97.5 %copy-start.8 = (bf16[128,1280]{1,0:T(8,128)(2,1)S(1)}, bf16[128,1280]{1,0:T(8,128)(2,1)}, u32[]{:S(2)}) copy-start(bf16[128,1280]{1,0:T(8,128)(2,1)} %get-tuple-element.18.mid_ref) | copy-start | bytes 983044
  213.8 3.9 %copy-start.7 = (bf16[2,320,1280]{2,1,0:T(8,128)(2,1)S(1)}, bf16[2,320,1280]{2,1,0:T(8,128)(2,1)}, u32[]{:S(2)}) copy-start(bf16[2,320,1280]{2,1,0:T(8,128)(2,1)} %get-tuple-element.28) | copy-start | bytes 4915204
  217.7 2.0 copy-start.6
